TPU v7x, 256 devices: a whole 4x4x8 slice. The times are simulated.
256 devices in a mesh: rows: 64 (over z, x, core), tm: 4 (over y).
Axes of the slice: x: 4, y: 4, z: 8, core: 2. Of those that a mesh axis runs over, the one named last changes fastest.
Arguments:
- frames: bfloat16 [16, 128, 256, 256], P('tm', 'rows'), may hold values from -45 to 45, as said below
- norm_gain: float32 [256], replicated, may hold values from 0.1 to 1.9
- conv_weight: bfloat16 [3, 3, 3, 256, 256], replicated, may hold values from -0.078125 to 0.078125
- conv_bias: float32 [256], replicated, may hold values from -3 to 3
- latent_grad: bfloat16 [16, 64, 128, 256], P('tm', None, 'rows'), may hold values from -6 to 6
Outputs:
- latent: bfloat16 [16, 64, 128, 256], P('tm', None, 'rows')
- frames_grad: bfloat16 [16, 128, 256, 256], P('tm', 'rows')
- weight_grad: float32 [3, 3, 3, 256, 256], P(None, None, None, 'tm')
- gain_grad: float32 [256], P('tm')
- bias_grad: float32 [256], P('tm')
Inputs may be any that keep to these rules, and one draw needn't show every extreme that they name: `frames`: features of the clip.
All inputs are finite; a program needn't handle non-finite values.
Results may differ from a plain program's by a relative error of at most 0.0045.
Values may be sent and summed in bfloat16 or wider, within the bound.
A program may use at most 128 MiB of HBM per device.

v0:
```python
import jax
import jax.numpy as jnp
from jax import lax
from jax.sharding import PartitionSpec as P


def shifted(value, axis, steps):
    count = lax.axis_size(axis)
    leading, last = (max(0, -steps), min(count, count - steps))
    return lax.ppermute(value, axis, [(source, source + steps) for source in range(leading, last)])


def contract_out(grad_piece, weight_tap):
    return lax.dot_general(
        grad_piece, weight_tap, (((1,), (1,)), ((), ())), preferred_element_type=jnp.float32
    )


def on_device(frames, norm_gain, conv_weight, conv_bias, latent_grad):
    signal = frames.astype(jnp.float32)
    inv_rms = lax.rsqrt(jnp.mean(signal * signal, axis=-1, keepdims=True) + 1e-06)
    unit = signal * inv_rms
    normed = unit * norm_gain
    hidden = jax.nn.silu(normed).astype(jnp.bfloat16)
    frame_count, row_count, col_count, channels = hidden.shape
    lat_rows = row_count // 2
    lat_cols = col_count // 2
    cached = shifted(hidden[frame_count - 2 :], "tm", 1)
    stacked = jnp.concatenate([cached, hidden], axis=0)
    row_under = shifted(stacked[:, :1], "rows", -1)
    extended = jnp.concatenate([stacked, row_under], axis=1)
    extended = jnp.pad(extended, ((0, 0), (0, 0), (0, 1), (0, 0)))
    grad_rows = lax.all_to_all(latent_grad, "rows", split_axis=1, concat_axis=2, tiled=True)
    grad_flat = grad_rows.reshape(-1, channels)
    running = jnp.zeros((frame_count * lat_rows * lat_cols, channels), jnp.float32)
    blocks = []
    for tap_t in range(3):
        for tap_r in range(3):
            for tap_c in range(3):
                window_piece = extended[
                    tap_t : tap_t + frame_count,
                    tap_r : tap_r + 2 * lat_rows : 2,
                    tap_c : tap_c + 2 * lat_cols : 2,
                ]
                window_piece = window_piece.reshape(-1, channels)
                running = running + jnp.dot(
                    window_piece,
                    conv_weight[tap_t, tap_r, tap_c],
                    preferred_element_type=jnp.float32,
                )
                blocks.append(
                    lax.dot_general(
                        window_piece,
                        grad_flat,
                        (((0,), (0,)), ((), ())),
                        preferred_element_type=jnp.float32,
                    )
                )
    latent_rows = (
        (running + conv_bias)
        .reshape(frame_count, lat_rows, lat_cols, channels)
        .astype(jnp.bfloat16)
    )
    latent = lax.all_to_all(latent_rows, "rows", split_axis=2, concat_axis=1, tiled=True)
    weight_local = jnp.stack(blocks).reshape(3, 3, 3, channels, channels)
    bias_local = jnp.sum(grad_flat.astype(jnp.float32), axis=0)
    spread_sum = jnp.zeros(
        (frame_count + 2, lat_rows + 1, 2, lat_cols + 1, 2, channels), jnp.float32
    )
    for tap_t in range(3):
        for tap_r in range(3):
            for tap_c in range(3):
                term = contract_out(grad_flat, conv_weight[tap_t, tap_r, tap_c])
                term = term.reshape(frame_count, lat_rows, lat_cols, channels)
                spread_sum = spread_sum.at[
                    tap_t : tap_t + frame_count,
                    tap_r // 2 : tap_r // 2 + lat_rows,
                    tap_r % 2,
                    tap_c // 2 : tap_c // 2 + lat_cols,
                    tap_c % 2,
                ].add(term)
    spread_sum = spread_sum.reshape(frame_count + 2, row_count + 2, col_count + 2, channels)[
        :, :, :col_count
    ]
    spilled = shifted(spread_sum[:, row_count : row_count + 1], "rows", 1)
    spread_sum = spread_sum[:, :row_count].at[:, :1].add(spilled)
    early_part = shifted(spread_sum[:2], "tm", -1)
    hidden_grad = spread_sum[2:].at[frame_count - 2 :].add(early_part)
    sigma = jax.nn.sigmoid(normed)
    normed_grad = hidden_grad * sigma * (1.0 + normed * (1.0 - sigma))
    gain_local = jnp.sum(normed_grad * unit, axis=(0, 1, 2))
    unit_grad = normed_grad * norm_gain
    frames_grad = inv_rms * (unit_grad - unit * jnp.mean(unit_grad * unit, axis=-1, keepdims=True))
    totals = lax.psum((weight_local, gain_local, bias_local), "rows")
    weight_grad, gain_grad, bias_grad = (
        lax.psum_scatter(totals[0], "tm", scatter_dimension=3, tiled=True),
        lax.psum_scatter(totals[1], "tm", scatter_dimension=0, tiled=True),
        lax.psum_scatter(totals[2], "tm", scatter_dimension=0, tiled=True),
    )
    return (latent, frames_grad.astype(jnp.bfloat16), weight_grad, gain_grad, bias_grad)


def solution(mesh):
    placed = (P("tm", "rows", None, None), P(), P(), P(), P("tm", None, "rows", None))
    return jax.shard_map(
        on_device,
        mesh=mesh,
        in_specs=placed,
        out_specs=(
            P("tm", None, "rows", None),
            P("tm", "rows", None, None),
            P(None, None, None, "tm", None),
            P("tm"),
            P("tm"),
        ),
        check_vma=False,
    )
```

profile of v0, /device:TPU:1, one launch (start us, length us, event | category | flops | bytes accessed | tf_op | source)
XLA Modules:
  0.0 572.6 jit_solution(2088232094615689766)
XLA Ops:
  8.3 25.8 %all_to_all.21 = bf16[4,64,2,256]{3,2,0,1:T(2,128)(2,1)S(1)} all-to-all(bf16[4,64,2,256]{3,2,0,1:T(2,128)(2,1)S(1)} %copy.17), channel_id=1, replica_groups=mesh['rows'=64,'tm'=4] {'rows'}, dimensions={1} | all-to-all | bytes 524288 | tf_op jit(solution)/shard_map/all_to_all | solution.py:33
  38.2 2.8 copy-done
  42.1 3.2 scatter-add.100
  51.0 3.2 scatter-add.105
  59.8 3.1 scatter-add.110
  68.7 3.1 scatter-add.115
  77.6 3.2 scatter-add.120
  86.5 3.2 scatter-add.125
  95.5 3.2 scatter-add.130
  104.4 3.2 scatter-add.135
  113.3 3.2 scatter-add.140
  116.4 10.5 %copy.19 = f32[6,2,2,129,2,256]{5,4,3,2,1,0:T(2,128)} copy(f32[6,2,2,129,2,256]{5,3,0,4,2,1:T(8,128)} %scatter-add.140) | data formatting | bytes 12681216 | tf_op jit(solution)/shard_map/scatter-add | solution.py:81
  126.9 8.5 %reshape.1745 = f32[6,4,258,256]{3,2,1,0:T(8,128)} reshape(f32[6,2,2,129,2,256]{5,4,3,2,1,0:T(2,128)} %copy.19) | data formatting | bytes 12681216 | tf_op jit(solution)/shard_map/reshape | solution.py:82
  137.1 2.8 collective-permute-start.2
  142.2 14.9 %collective-permute-done.2 = f32[6,1,256,256]{3,2,1,0:T(8,128)S(1)} collective-permute-done((f32[6,1,256,256]{3,2,1,0:T(8,128)S(1)}, f32[6,1,256,256]{3,2,1,0:T(8,128)S(1)}, u32[]{:S(2)}, u32[]{:S(2)}) %collective-permute-start.2) | collective-permute-done | bytes 1572896 | tf_op jit(solution)/shard_map/ppermute | solution.py:10
  160.7 13.7 %collective-permute-done.3 = f32[2,2,256,256]{3,2,1,0:T(8,128)S(1)} collective-permute-done((f32[2,2,256,256]{3,2,1,0:T(8,128)S(1)}, f32[2,2,256,256]{3,2,1,0:T(8,128)S(1)}, u32[]{:S(2)}, u32[]{:S(2)}) %collective-permute-start.3) | collective-permute-done | bytes 1048608 | tf_op jit(solution)/shard_map/ppermute | solution.py:10
  178.1 3.5 collective-permute-start
  181.6 6.1 %collective-permute-done = bf16[2,2,256,256]{3,2,1,0:T(8,128)(2,1)S(1)} collective-permute-done((bf16[2,2,256,256]{3,2,1,0:T(8,128)(2,1)S(1)}, bf16[2,2,256,256]{3,2,1,0:T(8,128)(2,1)S(1)}, u32[]{:S(2)}, u32[]{:S(2)}) %collective-permute-start) | collective-permute-done | bytes 524320 | tf_op jit(solution)/shard_map/ppermute | solution.py:10
  189.8 25.5 %collective-permute-done.1 = bf16[6,1,256,256]{3,2,1,0:T(8,128)(2,1)} collective-permute-done((bf16[6,1,256,256]{3,2,1,0:T(8,128)(2,1)S(1)}, bf16[6,1,256,256]{3,2,1,0:T(8,128)(2,1)}, u32[]{:S(2)}, u32[]{:S(2)}) %collective-permute-start.1) | collective-permute-done | bytes 786464 | tf_op jit(solution)/shard_map/ppermute | solution.py:10
  217.8 2.7 slice.1763
  220.5 2.6 slice.1761
  223.2 2.7 slice.1759
  225.8 2.7 slice.1757
  228.5 2.6 slice.1755
  231.1 2.6 slice.1753
  233.8 2.7 slice.1751
  236.5 2.6 slice.1749
  241.8 2.7 slice.1745
  244.4 2.6 slice.1743
  247.1 2.6 slice.1741
  249.7 2.7 slice.1739
  252.4 2.6 slice.1737
  257.7 2.7 slice.1733
  260.4 2.6 slice.1731
  263.0 2.6 slice.1729
  265.7 2.7 slice.1727
  268.3 2.7 slice.1725
  273.6 2.7 slice.1721
  276.3 2.6 slice.1719
  279.3 2.8 slice.1769
  294.0 2.8 copy-done.4
  330.0 41.6 %reduce-scatter.2.cloned.1.call-done = f32[3,3,3,64,256]{4,3,2,1,0:T(8,128)} async-done(((f32[3,3,3,256,256]{4,3,2,1,0:T(8,128)}), f32[3,3,3,64,256]{4,3,2,1,0:T(8,128)}) %reduce-scatter.2.cloned.1.call-update) | async-done | bytes 1769488 | tf_op jit(solution)/shard_map/reduce_scatter | solution.py:96
  371.6 5.7 %fusion.93 = bf16[512,256]{1,0:T(8,128)(2,1)S(1)} fusion(f32[512,256]{1,0:T(8,128)} %fusion.149, f32[512,256]{1,0:T(8,128)} %fusion.151, f32[512,256]{1,0:T(8,128)} %fusion.153, f32[512,256]{1,0:T(8,128)} %fusion.155, f32[512,256]{1,0:T(8,128)} %fusion.157, f32[512,256]{1,0:T(8,128)} %fusion.159, f32[512,256]{1,0:T(8,128)} %fusion.161, ...), kind=kOutput, calls=%fused_computation.125 | convolution fusion | flops 70778880 | bytes 14287872 | tf_op jit(solution)/shard_map/dot_general | solution.py:46
  378.3 10.7 %all-to-all-start = ((bf16[4,1,128,256]{3,0,1,2:T(4,128)(2,1)}), bf16[4,1,128,256]{3,0,1,2:T(4,128)(2,1)S(1)}, u32[]{:S(2)}, u32[]{:S(2)}) async-start(bf16[4,1,128,256]{3,0,1,2:T(4,128)(2,1)} %copy.16), calls=%async_computation | async-start | bytes 524288 | tf_op jit(solution)/shard_map/all_to_all | solution.py:64
  391.5 7.2 %all-reduce.5 = (f32[256]{0:T(256)S(1)}, f32[256]{0:T(256)S(1)}) all-reduce(f32[256]{0:T(256)S(1)} %get-tuple-element.363, f32[256]{0:T(256)S(1)} %convert_reduce_fusion), channel_id=3, replica_groups=mesh['rows'=64,'tm'=4] {'tm'}, use_global_device_ids=true, to_apply=%region_6.7.clone | all-reduce | flops 512 | bytes 4096
  398.9 126.0 %all-reduce.4 = (f32[64]{0:T(128)}, f32[64]{0:T(128)}) all-reduce(f32[64]{0:T(128)S(1)} %dynamic-slice.231, f32[64]{0:T(128)S(1)} %dynamic-slice.233), channel_id=1, replica_groups=mesh['rows'=64,'tm'=4] {'rows'}, use_global_device_ids=true, to_apply=%region_5.6 | all-reduce | flops 128 | bytes 1024 | tf_op jit(solution)/shard_map/psum | solution.py:94
  525.8 37.1 %all-reduce.8.cloned.1.call-done = f32[3,3,3,64,256]{4,3,2,1,0:T(8,128)} async-done(((f32[3,3,3,64,256]{4,3,2,1,0:T(8,128)}), f32[3,3,3,64,256]{4,3,2,1,0:T(8,128)}) %all-reduce.8.cloned.1.call-update) | async-done | bytes 1769488 | tf_op jit(solution)/shard_map/psum | solution.py:94
  562.9 2.9 copy.77
  (224 shorter events, 124.3 us)
Async XLA Ops:
  7.2 364.4 %reduce-scatter.2.cloned.1.call-start = ((), (), s32[]{:S(2)}) async-start(), calls=%async_computation.3 | async-start | bytes 8847360 | tf_op jit(solution)/shard_map/reduce_scatter | solution.py:96
  38.1 2.8 copy-start
  137.1 20.0 %collective-permute-start.2 = (f32[6,1,256,256]{3,2,1,0:T(8,128)S(1)}, f32[6,1,256,256]{3,2,1,0:T(8,128)S(1)}, u32[]{:S(2)}, u32[]{:S(2)}) collective-permute-start(f32[6,1,256,256]{3,2,1,0:T(8,128)S(1)} %slice.1830), channel_id=1, source_target_pairs={{0,4},{4,8},{8,12},{12,16},{16,20},{20,24},{24,28},{28,32},{32,36}... | collective-permute-start | bytes 4718600 | tf_op jit(solution)/shard_map/ppermute | solution.py:10
  142.2 18.0 %copy-start.3 = (bf16[4,2,256,256]{3,2,1,0:T(8,128)(2,1)S(1)}, bf16[4,2,256,256]{3,2,1,0:T(8,128)(2,1)}, u32[]{:S(2)}) copy-start(bf16[4,2,256,256]{3,2,1,0:T(8,128)(2,1)} %param.63) | copy-start | bytes 3145732
  158.9 15.5 %collective-permute-start.3 = (f32[2,2,256,256]{3,2,1,0:T(8,128)S(1)}, f32[2,2,256,256]{3,2,1,0:T(8,128)S(1)}, u32[]{:S(2)}, u32[]{:S(2)}) collective-permute-start(f32[2,2,256,256]{3,2,1,0:T(8,128)S(1)} %slice.1833), channel_id=1, source_target_pairs={{1,0},{2,1},{3,2},{5,4},{6,5},{7,6},{9,8},{10,9},{11,10},{13,12},{... | collective-permute-start | bytes 3145736 | tf_op jit(solution)/shard_map/ppermute | solution.py:10
  160.5 14.0 %copy-start.51 = (f32[256]{0:T(256)S(1)}, f32[256]{0:T(256)}, u32[]{:S(2)}) copy-start(f32[256]{0:T(256)} %param.64) | copy-start | bytes 3076
  178.0 9.7 %copy-start.2 = (bf16[4,2,256,256]{3,2,1,0:T(8,128)(2,1)}, bf16[4,2,256,256]{3,2,1,0:T(8,128)(2,1)S(1)}, u32[]{:S(2)}) copy-start(bf16[4,2,256,256]{3,2,1,0:T(8,128)(2,1)S(1)} %get-tuple-element.371) | copy-start | bytes 3145732
  178.1 9.6 %collective-permute-start = (bf16[2,2,256,256]{3,2,1,0:T(8,128)(2,1)S(1)}, bf16[2,2,256,256]{3,2,1,0:T(8,128)(2,1)S(1)}, u32[]{:S(2)}, u32[]{:S(2)}) collective-permute-start(bf16[2,2,256,256]{3,2,1,0:T(8,128)(2,1)S(1)} %slice.1802), channel_id=1, source_target_pairs={{0,1},{1,2},{2,3},{4,5},{5,6},{6,7},{8,9},{9,10},{10,11},{12,13},{... | collective-permute-start | bytes 1572872 | tf_op jit(solution)/shard_map/ppermute | solution.py:10
  187.8 27.6 %collective-permute-start.1 = (bf16[6,1,256,256]{3,2,1,0:T(8,128)(2,1)S(1)}, bf16[6,1,256,256]{3,2,1,0:T(8,128)(2,1)}, u32[]{:S(2)}, u32[]{:S(2)}) collective-permute-start(bf16[6,1,256,256]{3,2,1,0:T(8,128)(2,1)S(1)} %pad_maximum_fusion), channel_id=1, source_target_pairs={{4,0},{8,4},{12,8},{16,12},{20,16},{24,20},{28,24},{32,28},{36,32}... | collective-permute-start | bytes 2359304 | tf_op jit(solution)/shard_map/ppermute | solution.py:10
  217.4 76.1 %copy-start.6 = (bf16[4,1,128,256]{3,2,1,0:T(8,128)(2,1)}, bf16[4,1,128,256]{3,2,1,0:T(8,128)(2,1)S(1)}, u32[]{:S(2)}) copy-start(bf16[4,1,128,256]{3,2,1,0:T(8,128)(2,1)S(1)} %slice.1767) | copy-start | bytes 786436
  217.8 75.4 %copy-start.8 = (bf16[4,1,128,256]{3,2,1,0:T(8,128)(2,1)}, bf16[4,1,128,256]{3,2,1,0:T(8,128)(2,1)S(1)}, u32[]{:S(2)}) copy-start(bf16[4,1,128,256]{3,2,1,0:T(8,128)(2,1)S(1)} %slice.1765) | copy-start | bytes 786436
  279.3 9.4 %copy-start.5 = (bf16[4,1,128,256]{3,2,1,0:T(8,128)(2,1)}, bf16[4,1,128,256]{3,2,1,0:T(8,128)(2,1)S(1)}, u32[]{:S(2)}) copy-start(bf16[4,1,128,256]{3,2,1,0:T(8,128)(2,1)S(1)} %slice.1717) | copy-start | bytes 786436
  282.1 5.5 copy-start.46
  282.1 5.8 %copy-start.44 = (bf16[4,1,128,256]{3,2,1,0:T(8,128)(2,1)S(1)}, bf16[4,1,128,256]{3,2,1,0:T(8,128)(2,1)}, u32[]{:S(2)}) copy-start(bf16[4,1,128,256]{3,2,1,0:T(8,128)(2,1)} %slice.1729) | copy-start | bytes 786436
  282.1 6.1 %copy-start.42 = (bf16[4,1,128,256]{3,2,1,0:T(8,128)(2,1)S(1)}, bf16[4,1,128,256]{3,2,1,0:T(8,128)(2,1)}, u32[]{:S(2)}) copy-start(bf16[4,1,128,256]{3,2,1,0:T(8,128)(2,1)} %slice.1731) | copy-start | bytes 786436
  282.1 6.4 %copy-start.40 = (bf16[4,1,128,256]{3,2,1,0:T(8,128)(2,1)S(1)}, bf16[4,1,128,256]{3,2,1,0:T(8,128)(2,1)}, u32[]{:S(2)}) copy-start(bf16[4,1,128,256]{3,2,1,0:T(8,128)(2,1)} %slice.1733) | copy-start | bytes 786436
  282.1 6.7 %copy-start.38 = (bf16[4,1,128,256]{3,2,1,0:T(8,128)(2,1)S(1)}, bf16[4,1,128,256]{3,2,1,0:T(8,128)(2,1)}, u32[]{:S(2)}) copy-start(bf16[4,1,128,256]{3,2,1,0:T(8,128)(2,1)} %slice.1735) | copy-start | bytes 786436
  282.4 6.7 %copy-start.36 = (bf16[4,1,128,256]{3,2,1,0:T(8,128)(2,1)S(1)}, bf16[4,1,128,256]{3,2,1,0:T(8,128)(2,1)}, u32[]{:S(2)}) copy-start(bf16[4,1,128,256]{3,2,1,0:T(8,128)(2,1)} %slice.1737) | copy-start | bytes 786436
  283.7 5.6 copy-start.34
  285.0 4.7 copy-start.32
  286.3 3.7 copy-start.30
  294.0 2.8 copy-start.4
  296.9 266.0 %all-reduce.8.cloned.1.call-start = ((), (), s32[]{:S(2)}) async-start(), calls=%async_computation.4 | async-start | bytes 3538944 | tf_op jit(solution)/shard_map/psum | solution.py:94
  298.9 8.2 %copy-start.48 = (bf16[4,1,128,256]{3,2,1,0:T(8,128)(2,1)S(1)}, bf16[4,1,128,256]{3,2,1,0:T(8,128)(2,1)}, u32[]{:S(2)}) copy-start(bf16[4,1,128,256]{3,2,1,0:T(8,128)(2,1)} %slice.1725) | copy-start | bytes 786436
  298.9 9.2 %copy-start.47 = (bf16[4,1,128,256]{3,2,1,0:T(8,128)(2,1)S(1)}, bf16[4,1,128,256]{3,2,1,0:T(8,128)(2,1)}, u32[]{:S(2)}) copy-start(bf16[4,1,128,256]{3,2,1,0:T(8,128)(2,1)} %slice.1727) | copy-start | bytes 786436
  298.9 10.2 %copy-start.45 = (bf16[4,1,128,256]{3,2,1,0:T(8,128)(2,1)S(1)}, bf16[4,1,128,256]{3,2,1,0:T(8,128)(2,1)}, u32[]{:S(2)}) copy-start(bf16[4,1,128,256]{3,2,1,0:T(8,128)(2,1)} %slice.1729) | copy-start | bytes 786436
  298.9 11.3 %copy-start.43 = (bf16[4,1,128,256]{3,2,1,0:T(8,128)(2,1)S(1)}, bf16[4,1,128,256]{3,2,1,0:T(8,128)(2,1)}, u32[]{:S(2)}) copy-start(bf16[4,1,128,256]{3,2,1,0:T(8,128)(2,1)} %slice.1731) | copy-start | bytes 786436
  298.9 12.3 %copy-start.41 = (bf16[4,1,128,256]{3,2,1,0:T(8,128)(2,1)S(1)}, bf16[4,1,128,256]{3,2,1,0:T(8,128)(2,1)}, u32[]{:S(2)}) copy-start(bf16[4,1,128,256]{3,2,1,0:T(8,128)(2,1)} %slice.1733) | copy-start | bytes 786436
  301.0 11.3 %copy-start.39 = (bf16[4,1,128,256]{3,2,1,0:T(8,128)(2,1)S(1)}, bf16[4,1,128,256]{3,2,1,0:T(8,128)(2,1)}, u32[]{:S(2)}) copy-start(bf16[4,1,128,256]{3,2,1,0:T(8,128)(2,1)} %slice.1735) | copy-start | bytes 786436
  303.0 10.3 %copy-start.37 = (bf16[4,1,128,256]{3,2,1,0:T(8,128)(2,1)S(1)}, bf16[4,1,128,256]{3,2,1,0:T(8,128)(2,1)}, u32[]{:S(2)}) copy-start(bf16[4,1,128,256]{3,2,1,0:T(8,128)(2,1)} %slice.1737) | copy-start | bytes 786436
  305.0 9.4 %copy-start.35 = (bf16[4,1,128,256]{3,2,1,0:T(8,128)(2,1)S(1)}, bf16[4,1,128,256]{3,2,1,0:T(8,128)(2,1)}, u32[]{:S(2)}) copy-start(bf16[4,1,128,256]{3,2,1,0:T(8,128)(2,1)} %slice.1739) | copy-start | bytes 786436
  307.1 8.4 %copy-start.33 = (bf16[4,1,128,256]{3,2,1,0:T(8,128)(2,1)S(1)}, bf16[4,1,128,256]{3,2,1,0:T(8,128)(2,1)}, u32[]{:S(2)}) copy-start(bf16[4,1,128,256]{3,2,1,0:T(8,128)(2,1)} %slice.1741) | copy-start | bytes 786436
  308.1 8.4 %copy-start.31 = (bf16[4,1,128,256]{3,2,1,0:T(8,128)(2,1)S(1)}, bf16[4,1,128,256]{3,2,1,0:T(8,128)(2,1)}, u32[]{:S(2)}) copy-start(bf16[4,1,128,256]{3,2,1,0:T(8,128)(2,1)} %slice.1743) | copy-start | bytes 786436
  309.1 8.4 %copy-start.29 = (bf16[4,1,128,256]{3,2,1,0:T(8,128)(2,1)S(1)}, bf16[4,1,128,256]{3,2,1,0:T(8,128)(2,1)}, u32[]{:S(2)}) copy-start(bf16[4,1,128,256]{3,2,1,0:T(8,128)(2,1)} %slice.1745) | copy-start | bytes 786436
  310.2 8.4 %copy-start.27 = (bf16[4,1,128,256]{3,2,1,0:T(8,128)(2,1)S(1)}, bf16[4,1,128,256]{3,2,1,0:T(8,128)(2,1)}, u32[]{:S(2)}) copy-start(bf16[4,1,128,256]{3,2,1,0:T(8,128)(2,1)} %slice.1747) | copy-start | bytes 786436
  311.2 8.4 %copy-start.25 = (bf16[4,1,128,256]{3,2,1,0:T(8,128)(2,1)S(1)}, bf16[4,1,128,256]{3,2,1,0:T(8,128)(2,1)}, u32[]{:S(2)}) copy-start(bf16[4,1,128,256]{3,2,1,0:T(8,128)(2,1)} %slice.1749) | copy-start | bytes 786436
  312.3 8.3 %copy-start.23 = (bf16[4,1,128,256]{3,2,1,0:T(8,128)(2,1)S(1)}, bf16[4,1,128,256]{3,2,1,0:T(8,128)(2,1)}, u32[]{:S(2)}) copy-start(bf16[4,1,128,256]{3,2,1,0:T(8,128)(2,1)} %slice.1751) | copy-start | bytes 786436
  313.3 8.3 %copy-start.21 = (bf16[4,1,128,256]{3,2,1,0:T(8,128)(2,1)S(1)}, bf16[4,1,128,256]{3,2,1,0:T(8,128)(2,1)}, u32[]{:S(2)}) copy-start(bf16[4,1,128,256]{3,2,1,0:T(8,128)(2,1)} %slice.1753) | copy-start | bytes 786436
  314.4 8.3 %copy-start.19 = (bf16[4,1,128,256]{3,2,1,0:T(8,128)(2,1)S(1)}, bf16[4,1,128,256]{3,2,1,0:T(8,128)(2,1)}, u32[]{:S(2)}) copy-start(bf16[4,1,128,256]{3,2,1,0:T(8,128)(2,1)} %slice.1755) | copy-start | bytes 786436
  315.4 8.3 %copy-start.17 = (bf16[4,1,128,256]{3,2,1,0:T(8,128)(2,1)S(1)}, bf16[4,1,128,256]{3,2,1,0:T(8,128)(2,1)}, u32[]{:S(2)}) copy-start(bf16[4,1,128,256]{3,2,1,0:T(8,128)(2,1)} %slice.1757) | copy-start | bytes 786436
  316.4 8.3 %copy-start.15 = (bf16[4,1,128,256]{3,2,1,0:T(8,128)(2,1)S(1)}, bf16[4,1,128,256]{3,2,1,0:T(8,128)(2,1)}, u32[]{:S(2)}) copy-start(bf16[4,1,128,256]{3,2,1,0:T(8,128)(2,1)} %slice.1759) | copy-start | bytes 786436
  317.5 8.3 %copy-start.13 = (bf16[4,1,128,256]{3,2,1,0:T(8,128)(2,1)S(1)}, bf16[4,1,128,256]{3,2,1,0:T(8,128)(2,1)}, u32[]{:S(2)}) copy-start(bf16[4,1,128,256]{3,2,1,0:T(8,128)(2,1)} %slice.1761) | copy-start | bytes 786436
  318.5 8.3 %copy-start.11 = (bf16[4,1,128,256]{3,2,1,0:T(8,128)(2,1)S(1)}, bf16[4,1,128,256]{3,2,1,0:T(8,128)(2,1)}, u32[]{:S(2)}) copy-start(bf16[4,1,128,256]{3,2,1,0:T(8,128)(2,1)} %slice.1763) | copy-start | bytes 786436
  319.6 8.3 %copy-start.9 = (bf16[4,1,128,256]{3,2,1,0:T(8,128)(2,1)S(1)}, bf16[4,1,128,256]{3,2,1,0:T(8,128)(2,1)}, u32[]{:S(2)}) copy-start(bf16[4,1,128,256]{3,2,1,0:T(8,128)(2,1)} %copy-done.8) | copy-start | bytes 786436
  320.6 8.3 %copy-start.7 = (bf16[4,1,128,256]{3,2,1,0:T(8,128)(2,1)S(1)}, bf16[4,1,128,256]{3,2,1,0:T(8,128)(2,1)}, u32[]{:S(2)}) copy-start(bf16[4,1,128,256]{3,2,1,0:T(8,128)(2,1)} %copy-done.6) | copy-start | bytes 786436
  323.7 47.9 %copy-start.52 = (f32[256]{0:T(256)S(1)}, f32[256]{0:T(256)}, u32[]{:S(2)}) copy-start(f32[256]{0:T(256)} %param.66) | copy-start | bytes 3076
  371.6 17.4 %copy-start.53 = (u32[256]{0:T(256)S(1)}, u32[256]{0:T(256)}, u32[]{:S(2)}) copy-start(u32[256]{0:T(256)} %constant.1073) | copy-start | bytes 3076
  378.3 146.6 %all-to-all-start = ((bf16[4,1,128,256]{3,0,1,2:T(4,128)(2,1)}), bf16[4,1,128,256]{3,0,1,2:T(4,128)(2,1)S(1)}, u32[]{:S(2)}, u32[]{:S(2)}) async-start(bf16[4,1,128,256]{3,0,1,2:T(4,128)(2,1)} %copy.16), calls=%async_computation | async-start | bytes 524288 | tf_op jit(solution)/shard_map/all_to_all | solution.py:64
  (13 other events, 31.8 us)
Sparse Core Ops, SparseCore 0:
  297.0 74.5 reduce-scatter.1
  375.0 187.8 all-reduce.7
where the time goes:
time: 575 us; the launch traced here: 573 us
  blocking collectives  159 us (28%)
  waiting for transfers between devices  139 us (24%)
  local copies, waits for them, and re-layouts  132 us (23%)
  matrix products  97.4 us (17%)
  starting transfers between devices  20.6 us (4%)
  between operations  15.6 us (3%)
  other arithmetic  8.64 us (2%)
    psum x1, blocking collectives, on_device(): totals = lax.psum((weight_local, gain_local, bias_local), 'rows')  126 us
    slice x27, local copies, waits for them, and re-layouts, on_device(): extended[tap_t:tap_t + frame_count, tap_r:tap_r + 2 * lat_rows:2, tap_c:t...  65 us
    ppermute x4, waiting for transfers between devices, shifted(): lax.ppermute(value, axis, [(source, source + steps) for source in range(l...  60.2 us
    dot_general x27, matrix products, contract_out(): lax.dot_general(grad_piece, weight_tap, (((1,), (1,)), ((), ())), preferr...  49.4 us
    reduce_scatter x1, waiting for transfers between devices, on_device(): lax.psum_scatter(totals[0], 'tm', scatter_dimension=3, tiled=True)  41.6 us
    scatter-add x11, local copies, waits for them, and re-layouts, on_device(): spread_sum = spread_sum.at[tap_t:tap_t + frame_count, tap_r // 2:tap_r //...  39.5 us
    psum x1, waiting for transfers between devices, on_device(): totals = lax.psum((weight_local, gain_local, bias_local), 'rows')  37.1 us
    dot_general x27, matrix products, on_device(): jnp.dot(window_piece, conv_weight[tap_t, tap_r, tap_c], preferred_element...  36.7 us
  transfers between devices with their start and end apart: 7, of which 6 were waited for; matrix products, arithmetic and copies ran while one was open for 8% of the time, Pallas kernels for 0%

commit v1 on v0

v1 whole, which is shorter than its diff:
```python
import functools

import jax
import jax.numpy as jnp
from jax import lax
from jax.experimental import pallas as pl
from jax.experimental.pallas import tpu as pltpu
from jax.sharding import PartitionSpec as P

F32 = jnp.float32
BF16 = jnp.bfloat16
MESH = pl.DeviceIdType.MESH
EPS = 1e-06
NX, NZ, NY = 4, 8, 4
CHUNKS, TAPS = 7, 4


def shifted(value, axis, steps):
    count = lax.axis_size(axis)
    leading, last = (max(0, -steps), min(count, count - steps))
    return lax.ppermute(value, axis, [(source, source + steps) for source in range(leading, last)])


def dot_nt(left, right):
    return lax.dot_general(left, right, (((1,), (1,)), ((), ())), preferred_element_type=F32)


def dot_nn(left, right):
    return lax.dot_general(left, right, (((1,), (0,)), ((), ())), preferred_element_type=F32)


def inverse_rms(signal):
    return lax.rsqrt(jnp.mean(signal * signal, axis=-1, keepdims=True) + EPS)


def section_kernel(
    frames, early, below, gain, weight, bias, grad, grad_above,
    latent, frames_grad, parts,
    columns, turned, grad_next, spread, tile, gain_sum,
):
    gain_row = gain[...]
    row_at = lax.broadcasted_iota(jnp.int32, (128, 256), 0)

    def hidden_tile(source, at, row, keep):
        for piece in range(4):
            rows = pl.ds(piece * 64, 64)
            signal = source[rows, :].astype(F32)
            normed = signal * inverse_rms(signal) * gain_row
            hidden = normed / (1.0 + jnp.exp(-normed))
            tile[row, 0, rows, :] = hidden[:, :128]
            tile[row, 1, rows, :] = hidden[:, 128:]
        even = jnp.concatenate([tile[row, half, pl.ds(0, 128, stride=2), :] for half in range(2)], axis=1)
        odd = jnp.concatenate([tile[row, half, pl.ds(1, 128, stride=2), :] for half in range(2)], axis=1)
        after = jnp.where(row_at == 127, 0.0, pltpu.roll(even, 127, 0))
        where = pl.ds(pl.multiple_of(at * 128, 128), 128)
        columns[where, pl.ds(row * 768, 256)] = even.astype(BF16)
        columns[where, pl.ds(row * 768 + 256, 256)] = odd.astype(BF16)
        columns[where, pl.ds(row * 768 + 512, 256)] = after.astype(BF16)
        if keep:
            lanes = pl.ds(pl.multiple_of((at - 2) * 128, 128), 128)
            turned[2 * row, :, lanes] = even.T.astype(BF16)
            turned[2 * row + 1, :, lanes] = odd.T.astype(BF16)

    @pl.loop(0, 2)
    def _(at):
        hidden_tile(early.at[at, 0], at, 0, False)
        hidden_tile(early.at[at, 1], at, 1, False)

    @pl.loop(2, 6)
    def _(at):
        hidden_tile(frames.at[at - 2, 0], at, 0, True)
        hidden_tile(frames.at[at - 2, 1], at, 1, True)

    @pl.loop(0, 6)
    def _(at):
        hidden_tile(below.at[at], at, 2, False)
        where = pl.ds(pl.multiple_of(at * 128, 128), 128)
        for which, source in enumerate((grad, grad_above)):
            moved = pltpu.roll(source[where, :].astype(F32), 1, 0)
            grad_next[which, where, :] = jnp.where(row_at == 0, 0.0, moved).astype(BF16)

    spread[0] = jnp.broadcast_to(bias[...], (512, 256))

    @pl.loop(0, 3)
    def _(tap):
        where = pl.ds(pl.multiple_of(tap * 128, 128), 512)
        spread[0] += dot_nn(columns[where, :], weight[tap].reshape(2304, 256))

    latent[...] = spread[0].astype(BF16)
    spread[...] = jnp.zeros_like(spread)
    gain_sum[...] = jnp.zeros_like(gain_sum)

    @pl.loop(0, 3)
    def _(tap):
        where = pl.ds(pl.multiple_of((2 - tap) * 128, 128), 512)
        here, here_next = grad[where, :], grad_next[0, where, :]
        above, above_next = grad_above[where, :], grad_next[1, where, :]
        spread[0] += dot_nt(here, weight[tap, 0]) + dot_nt(here_next, weight[tap, 2])
        spread[0] += dot_nt(above, weight[tap, 6]) + dot_nt(above_next, weight[tap, 8])
        spread[1] += dot_nt(here, weight[tap, 1]) + dot_nt(above, weight[tap, 7])
        spread[2] += dot_nt(here, weight[tap, 3]) + dot_nt(here_next, weight[tap, 5])
        spread[3] += dot_nt(here, weight[tap, 4])
        for spot in range(9):
            tap_r, tap_c = spot // 3, spot % 3
            left = turned[2 * (tap_r % 2) + tap_c % 2]
            if tap_r == 2:
                right = above_next if tap_c == 2 else above
            else:
                right = here_next if tap_c == 2 else here
            block = dot_nn(left, right).astype(BF16)
            parts[0, tap * 9 + spot] = block[:, :128]
            parts[1, tap * 9 + spot] = block[:, 128:]

    @pl.loop(0, 4)
    def _(at):
        where = pl.ds(pl.multiple_of(at * 128, 128), 128)
        for row in range(2):
            for half in range(2):
                lanes = pl.ds(half * 128, 128)
                tile[row, half, pl.ds(0, 128, stride=2), :] = spread[2 * row, where, lanes]
                tile[row, half, pl.ds(1, 128, stride=2), :] = spread[2 * row + 1, where, lanes]
            for piece in range(4):
                rows = pl.ds(piece * 64, 64)
                signal = frames[at, row, rows, :].astype(F32)
                inv = inverse_rms(signal)
                unit = signal * inv
                normed = unit * gain_row
                sigma = 1.0 / (1.0 + jnp.exp(-normed))
                arrived = jnp.concatenate([tile[row, half, rows, :] for half in range(2)], axis=1)
                normed_grad = arrived * sigma * (1.0 + normed * (1.0 - sigma))
                gain_sum[...] += jnp.sum((normed_grad * unit).reshape(8, 8, 256), axis=0)
                unit_grad = normed_grad * gain_row
                mean = jnp.mean(unit_grad * unit, axis=-1, keepdims=True)
                frames_grad[at, row, rows, :] = (inv * (unit_grad - unit * mean)).astype(BF16)

    gain_local = jnp.sum(gain_sum[...], axis=0, keepdims=True)
    bias_local = jnp.sum(grad[pl.ds(0, 512), :].astype(F32), axis=0, keepdims=True)
    spot = lax.broadcasted_iota(jnp.int32, (256, 256), 0) % 64
    gain_rest = gain_local - gain_local.astype(BF16).astype(F32)
    bias_rest = bias_local - bias_local.astype(BF16).astype(F32)
    small = jnp.where(spot == 0, gain_local, jnp.where(spot == 1, bias_local, 0.0))
    small = jnp.where(spot == 2, gain_rest, jnp.where(spot == 3, bias_rest, small)).astype(BF16)
    parts[0, 27] = small[:, :128]
    parts[1, 27] = small[:, 128:]


def section(frames, early, below, gain, weight, bias, grad, grad_above):
    return pl.pallas_call(
        section_kernel,
        out_shape=(
            jax.ShapeDtypeStruct((512, 256), BF16),
            jax.ShapeDtypeStruct((4, 2, 256, 256), BF16),
            jax.ShapeDtypeStruct((2, 28, 256, 128), BF16),
        ),
        in_specs=[pl.BlockSpec(memory_space=pltpu.VMEM)] * 8,
        out_specs=[pl.BlockSpec(memory_space=pltpu.VMEM)] * 3,
        scratch_shapes=[
            pltpu.VMEM((768, 2304), BF16),
            pltpu.VMEM((4, 256, 512), BF16),
            pltpu.VMEM((2, 768, 256), BF16),
            pltpu.VMEM((4, 512, 256), F32),
            pltpu.VMEM((3, 2, 256, 128), F32),
            pltpu.VMEM((8, 256), F32),
        ],
        cost_estimate=pl.CostEstimate(flops=5_500_000_000, bytes_accessed=12_000_000, transcendentals=2_000_000),
    )(frames, early, below, gain, weight, bias, grad, grad_above)


def reduce_kernel(
    parts, latent, result, latent_out, other, mine, first_plus, first_minus, second_plus, second_minus,
    mid, first_plus2, first_minus2, second_plus2, second_minus2,
    low, arrive, total, block, latent_mid,
    core_sem, ring_sem, ring2_sem, z_sem, zback_sem, x_sem, pair_sem, lat_sem,
):
    rows_at = lax.axis_index("rows")
    y = lax.axis_index("tm")
    core, x, z = rows_at % 2, (rows_at // 2) % NX, rows_at // (2 * NX)
    slab = rows_at % (2 * NX)

    def row_of(z_at, x_at, core_at):
        return z_at * (2 * NX) + x_at * 2 + core_at

    sibling = (row_of(z, x, 1 - core), y)

    def along(axis, step):
        if axis == "y":
            return (rows_at, (y + step) % NY)
        if axis == "x":
            return (row_of(z, (x + step) % NX, core), y)
        if axis == "slab":
            return (z * (2 * NX) + (slab + step) % (2 * NX), y)
        return (row_of((z + step) % NZ, x, core), y)

    barrier = pltpu.get_barrier_semaphore()
    friends = [along("slab", step) for step in range(1, 2 * NX)]
    friends += [along("y", 1), along("y", 3)]
    friends += [along("z", step) for step in range(1, NZ)]
    for friend in friends:
        pl.semaphore_signal(barrier, inc=1, device_id=friend, device_id_type=MESH)
    pl.semaphore_wait(barrier, len(friends))

    def copy_to(source, target, sems, at, device):
        return pltpu.make_async_remote_copy(
            src_ref=source, dst_ref=target, send_sem=sems.at[(0, *at)], recv_sem=sems.at[(1, *at)],
            device_id=device, device_id_type=MESH,
        )

    def send(*args):
        copy = copy_to(*args)
        copy.start()
        return copy

    pair = []
    for chunk in range(CHUNKS):
        spots = pl.ds(chunk * TAPS, TAPS)
        pair.append(send(parts.at[1 - core, spots], other.at[spots], core_sem, (chunk,), sibling))
    outer = [
        send(latent.at[(z + step) % NZ], latent_mid.at[z], lat_sem, (0, step), along("z", step))
        for step in range(1, NZ)
    ]
    latent_mid[z] = latent[z]
    started = pair + outer

    def axes_of(chunk):
        return ("y", "x") if chunk % 2 == 0 else ("x", "y")

    def here(axis, step):
        return (y + step) % NY if axis == "y" else (x + step) % NX

    def piece(ref, chunk, stage, at, taps):
        if stage == 0 and axes_of(chunk)[0] == "x":
            return ref.at[chunk, taps, slice(None), at]
        return ref.at[chunk, taps, at]

    FIRST, LAST, ALL = pl.ds(0, 2), pl.ds(2, 2), pl.ds(0, 4)
    banks = (
        (mine, first_plus, first_minus, second_plus, second_minus, ring_sem, BF16),
        (mid, first_plus2, first_minus2, second_plus2, second_minus2, ring2_sem, F32),
    )

    def ring_open(chunk, stage):
        source, plus, minus, _, _, sems, _ = banks[stage]
        axis = axes_of(chunk)[stage]
        far = here(axis, 2)
        return [
            send(piece(source, chunk, stage, far, FIRST), plus.at[chunk], sems, (chunk, 0), along(axis, 1)),
            send(piece(source, chunk, stage, far, LAST), minus.at[chunk], sems, (chunk, 1), along(axis, 3)),
        ]

    def ring_next(chunk, stage, opened):
        source, plus, minus, plus_in, minus_in, sems, kind = banks[stage]
        axis = axes_of(chunk)[stage]
        opened[0].wait_recv()
        ahead = piece(source, chunk, stage, here(axis, 1), FIRST)
        ahead[...] = (ahead[...].astype(F32) + plus[chunk].astype(F32)).astype(kind)
        one = send(piece(source, chunk, stage, here(axis, 1), ALL), plus_in.at[chunk], sems, (chunk, 2), along(axis, 1))
        opened[1].wait_recv()
        behind = piece(source, chunk, stage, here(axis, 3), LAST)
        behind[...] = (behind[...].astype(F32) + minus[chunk].astype(F32)).astype(kind)
        two = send(piece(source, chunk, stage, here(axis, 3), ALL), minus_in.at[chunk], sems, (chunk, 3), along(axis, 3))
        return [one, two]

    def ring_close(chunk, stage, sent):
        source, _, _, plus_in, minus_in, _, _ = banks[stage]
        axis = axes_of(chunk)[stage]
        sent[0].wait_recv()
        sent[1].wait_recv()
        own = piece(source, chunk, stage, here(axis, 0), ALL)[...].astype(F32)
        (mid, low)[stage][chunk] = own + plus_in[chunk].astype(F32) + minus_in[chunk].astype(F32)

    def to_owner(chunk):
        step = (chunk - z + NZ) % NZ
        return pltpu.make_async_remote_copy(
            src_ref=low.at[chunk], dst_ref=arrive.at[step], send_sem=z_sem.at[0, chunk], recv_sem=z_sem.at[1, step],
            device_id=(row_of(chunk, x, core), y), device_id_type=MESH,
        )

    opened, sent, opened2, sent2 = {}, {}, {}, {}
    for chunk in range(CHUNKS):
        pair[chunk].wait_recv()
        spots = pl.ds(chunk * TAPS, TAPS)
        summed = parts[core, spots].astype(F32) + other[spots].astype(F32)
        mine[chunk] = summed.astype(BF16).reshape(TAPS, NY, NX, 16, 128)
        opened[chunk] = ring_open(chunk, 0)
    for chunk in range(CHUNKS):
        sent[chunk] = ring_next(chunk, 0, opened[chunk])
    for copy in outer:
        copy.wait_recv()
    inner = [
        send(latent_mid.at[:, (slab + step) % (2 * NX)], latent_out.at[:, slab], lat_sem, (1, step), along("slab", step))
        for step in range(1, 2 * NX)
    ]
    latent_out[:, slab] = latent_mid[:, slab]
    for chunk in range(CHUNKS):
        ring_close(chunk, 0, sent[chunk])
        opened2[chunk] = ring_open(chunk, 1)
    for chunk in range(CHUNKS):
        sent2[chunk] = ring_next(chunk, 1, opened2[chunk])
    for chunk in range(CHUNKS):
        ring_close(chunk, 1, sent2[chunk])

        @pl.when(z != chunk)
        def _():
            to_owner(chunk).start()

    started += inner
    for table in (opened, sent, opened2, sent2):
        for chunk in range(CHUNKS):
            started += table[chunk]

    def back(step):
        return copy_to(total.at[z], total.at[z], zback_sem, (step,), along("z", step))

    @pl.when(z < CHUNKS)
    def _():
        summed = low[z]
        for step in range(1, NZ):
            pltpu.make_async_remote_copy(
                src_ref=low.at[0], dst_ref=arrive.at[step], send_sem=z_sem.at[0, 0], recv_sem=z_sem.at[1, step],
                device_id=sibling, device_id_type=MESH,
            ).wait_recv()
            summed += arrive[step]
        total[z] = summed.astype(BF16)
        for step in range(1, NZ):
            back(step).start()

    right, left, across = (x + 1) % NX, (x + 3) % NX, (x + 2) % NX
    order = (0, 1, 7, 2, 6, 3, 5, 4)

    def to_right(step, at):
        return copy_to(total.at[at], block.at[x, at], x_sem, (0, step), along("x", 1))

    def to_left(step, at):
        return copy_to(total.at[at], block.at[x, at], x_sem, (1, step), along("x", 3))

    def on_right(step, at):
        half = block.at[left, at, FIRST]
        return copy_to(half, half, x_sem, (2, step), along("x", 1))

    def on_left(step, at):
        half = block.at[right, at, LAST]
        return copy_to(half, half, x_sem, (3, step), along("x", 3))

    def across_core(which, step, at):
        source = total.at[at] if which == 0 else block.at[(left, right, across)[which - 1], at]
        where = (x, left, right, across)[which]
        return copy_to(source, result.at[core, where, at], pair_sem, (which, step), sibling)

    def each(body):
        for step in order:
            at = (z - step + NZ) % NZ

            @pl.when(at < CHUNKS)
            def _():
                body(step, at)

    def fan_one(step, at):
        if step:
            back(step).wait_recv()
        to_right(step, at).start()
        to_left(step, at).start()
        across_core(0, step, at).start()
        result[core, x, at] = total[at]

    def fan_two(step, at):
        to_right(step, at).wait_recv()
        on_right(step, at).start()
        across_core(1, step, at).start()
        result[core, left, at] = block[left, at]
        to_left(step, at).wait_recv()
        on_left(step, at).start()
        across_core(2, step, at).start()
        result[core, right, at] = block[right, at]

    def fan_three(step, at):
        on_right(step, at).wait_recv()
        on_left(step, at).wait_recv()
        across_core(3, step, at).start()
        result[core, across, at] = block[across, at]

    def fan_last(step, at):
        for which in range(4):
            across_core(which, step, at).wait()
        to_right(step, at).wait_send()
        to_left(step, at).wait_send()
        on_right(step, at).wait_send()
        on_left(step, at).wait_send()

    each(fan_one)
    each(fan_two)
    each(fan_three)
    for copy in inner:
        copy.wait_recv()
    for copy in started:
        copy.wait_send()
    each(fan_last)

    for chunk in range(CHUNKS):

        @pl.when(z != chunk)
        def _():
            to_owner(chunk).wait_send()

    @pl.when(z < CHUNKS)
    def _():
        for step in range(1, NZ):
            back(step).wait_send()


def reduce_all(parts, latent):
    dma = pltpu.SemaphoreType.DMA
    return pl.pallas_call(
        reduce_kernel,
        out_shape=(
            jax.ShapeDtypeStruct((2, NX, CHUNKS, TAPS, 16, 128), BF16),
            jax.ShapeDtypeStruct((NZ, 2 * NX, 8, 256), BF16),
        ),
        in_specs=[pl.BlockSpec(memory_space=pltpu.VMEM)] * 2,
        out_specs=[pl.BlockSpec(memory_space=pltpu.VMEM)] * 2,
        scratch_shapes=[
            pltpu.VMEM((CHUNKS * TAPS, 256, 128), BF16),
            pltpu.VMEM((CHUNKS, TAPS, NY, NX, 16, 128), BF16),
            pltpu.VMEM((CHUNKS, 2, 4, 16, 128), BF16),
            pltpu.VMEM((CHUNKS, 2, 4, 16, 128), BF16),
            pltpu.VMEM((CHUNKS, TAPS, 4, 16, 128), BF16),
            pltpu.VMEM((CHUNKS, TAPS, 4, 16, 128), BF16),
            pltpu.VMEM((CHUNKS, TAPS, 4, 16, 128), F32),
            pltpu.VMEM((CHUNKS, 2, 16, 128), F32),
            pltpu.VMEM((CHUNKS, 2, 16, 128), F32),
            pltpu.VMEM((CHUNKS, TAPS, 16, 128), F32),
            pltpu.VMEM((CHUNKS, TAPS, 16, 128), F32),
            pltpu.VMEM((NZ, TAPS, 16, 128), F32),
            pltpu.VMEM((NZ, TAPS, 16, 128), F32),
            pltpu.VMEM((NZ, TAPS, 16, 128), BF16),
            pltpu.VMEM((NX, NZ, TAPS, 16, 128), BF16),
            pltpu.VMEM((NZ, 2 * NX, 8, 256), BF16),
            dma((2, CHUNKS)),
            dma((2, CHUNKS, 4)),
            dma((2, CHUNKS, 4)),
            dma((2, NZ)),
            dma((2, NZ)),
            dma((2, 4, NZ)),
            dma((2, 4, NZ)),
            dma((2, 2, NZ)),
        ],
        compiler_params=pltpu.CompilerParams(collective_id=1, has_side_effects=True),
        cost_estimate=pl.CostEstimate(flops=20_000_000, bytes_accessed=6_000_000, transcendentals=0),
    )(parts, latent)


def finish_kernel(total, weight_grad, small):
    for core in range(2):
        lanes = pl.ds(core * 128, 128)
        for x in range(NX):
            rows = pl.ds(x * 16, 16)
            for tap in range(27):
                weight_grad[tap, rows, lanes] = total[core, x, tap // TAPS, tap % TAPS].astype(F32)
        sums = total[core, 0, 6, 3].astype(F32)
        small[:, lanes] = sums[0:8] + pltpu.roll(sums[0:8], 6, 0)


def finish(total):
    return pl.pallas_call(
        finish_kernel,
        out_shape=(jax.ShapeDtypeStruct((27, 64, 256), F32), jax.ShapeDtypeStruct((8, 256), F32)),
        in_specs=[pl.BlockSpec(memory_space=pltpu.VMEM)],
        out_specs=[pl.BlockSpec(memory_space=pltpu.VMEM)] * 2,
    )(total)


def on_device(frames, norm_gain, conv_weight, conv_bias, latent_grad):
    early = shifted(frames[2:], "tm", 1)
    below = shifted(jnp.concatenate([early[:, 0], frames[:, 0]], axis=0), "rows", -1)
    grad_rows = lax.all_to_all(latent_grad, "rows", split_axis=1, concat_axis=2, tiled=True)
    grad_rows = grad_rows.reshape(512, 256)
    grad = jnp.concatenate([grad_rows, shifted(grad_rows[:256], "tm", -1)], axis=0)
    grad_above = shifted(grad, "rows", 1)
    latent_rows, frames_grad, parts = section(
        frames, early, below, norm_gain.reshape(1, 256), conv_weight.reshape(3, 9, 256, 256),
        conv_bias.reshape(1, 256), grad, grad_above,
    )
    blocks = latent_rows.reshape(4, 64, 2, 256).transpose(1, 0, 2, 3).reshape(NZ, 2 * NX, 8, 256)
    total, latent_blocks = reduce_all(parts, blocks)
    latent = latent_blocks.reshape(64, 4, 2, 256).transpose(1, 0, 2, 3)
    weight_grad, small = finish(total)
    own = lax.dynamic_slice_in_dim(small, lax.axis_index("tm") * 64, 64, axis=1)
    return latent, frames_grad, weight_grad.reshape(3, 3, 3, 64, 256), own[0], own[1]


def solution(mesh):
    placed = (P("tm", "rows", None, None), P(), P(), P(), P("tm", None, "rows", None))
    return jax.shard_map(
        on_device,
        mesh=mesh,
        in_specs=placed,
        out_specs=(
            P("tm", None, "rows", None),
            P("tm", "rows", None, None),
            P(None, None, None, "tm", None),
            P("tm"),
            P("tm"),
        ),
        check_vma=False,
    )
```

time: 575 us -> 128 us (0.22)
  blocking collectives: 159 us -> 0 us
  waiting for transfers between devices: 139 us -> 18.4 us
  local copies, waits for them, and re-layouts: 132 us -> 11.6 us
  matrix products: 97.4 us -> 0 us
  Pallas kernels: 0 us -> 73.2 us
  between operations: 15.6 us -> 0.79 us
  other arithmetic: 8.64 us -> 0.07 us
    psum x1 -> x0, blocking collectives: 126 us -> none  [on_device(): totals = lax.psum((weight_local, gain_local, bias_local), 'rows')]
    dot_general x81 -> x0, matrix products: 97.4 us -> none  [the longest x27 49.4 us: contract_out(): lax.dot_general(grad_piece, weight_tap, (((1,), (1,)), ((), ())), preferr...]
    pallas_call x0 -> x3, Pallas kernels: none -> 73.2 us  [the longest x1 52.9 us: reduce_all(): pl.pallas_call(reduce_kernel, out_shape=(jax.ShapeDtypeStruct((2, NX, CHU...]
    slice x32 -> x4, local copies, waits for them, and re-layouts: 69.1 us -> 1.32 us  [the longest x1 1.08 us: on_device(): early = shifted(frames[2:], 'tm', 1)]
    ppermute x4, waiting for transfers between devices: 60.2 us -> 8.92 us  [shifted(): lax.ppermute(value, axis, [(source, source + steps) for source in range(l...]
    reduce_scatter x1 -> x0, waiting for transfers between devices: 41.6 us -> none  [on_device(): lax.psum_scatter(totals[0], 'tm', scatter_dimension=3, tiled=True)]
    scatter-add x11 -> x0, local copies, waits for them, and re-layouts: 39.5 us -> none  [on_device(): spread_sum = spread_sum.at[tap_t:tap_t + frame_count, tap_r // 2:tap_r //...]
    psum x1 -> x0, waiting for transfers between devices: 37.1 us -> none  [on_device(): totals = lax.psum((weight_local, gain_local, bias_local), 'rows')]
  transfers between devices with their start and end apart: 7 -> 5, of which waited for: 6 -> 3; matrix products, arithmetic and copies ran while one was open for 8% -> 3% of each run, Pallas kernels for 0% -> 0%
where the time goes in v1:
time: 128 us
  Pallas kernels  73.2 us (57%)
  starting transfers between devices  23.6 us (18%)
  waiting for transfers between devices  18.4 us (14%)
  local copies, waits for them, and re-layouts  11.6 us (9%)
    pallas_call x1, Pallas kernels, reduce_all(): pl.pallas_call(reduce_kernel, out_shape=(jax.ShapeDtypeStruct((2, NX, CHU...  52.9 us
    pallas_call x1, Pallas kernels, section(): pl.pallas_call(section_kernel, out_shape=(jax.ShapeDtypeStruct((512, 256)...  17.7 us
    all_to_all x1, starting transfers between devices, on_device(): lax.all_to_all(latent_grad, 'rows', split_axis=1, concat_axis=2, tiled=True)  12.4 us
    ppermute x4, starting transfers between devices, shifted(): lax.ppermute(value, axis, [(source, source + steps) for source in range(l...  11.1 us
    all_to_all x1, waiting for transfers between devices, on_device(): lax.all_to_all(latent_grad, 'rows', split_axis=1, concat_axis=2, tiled=True)  9.5 us
    ppermute x4, waiting for transfers between devices, shifted(): lax.ppermute(value, axis, [(source, source + steps) for source in range(l...  8.92 us
    unnamed x7, local copies, waits for them, and re-layouts  2.77 us
  transfers between devices with their start and end apart: 5, of which 3 were waited for; matrix products, arithmetic and copies ran while one was open for 3% of the time, Pallas kernels for 0%

profile of v1, /device:TPU:1, one launch (start us, length us, event | category | flops | bytes accessed | tf_op | source)
XLA Modules:
  0.0 127.6 jit_solution(13738614926081839566)
XLA Ops:
  0.6 1.1 slice.21
  1.8 4.1 %collective-permute-start = (bf16[2,2,256,256]{3,2,0,1:T(8,128)(2,1)S(1)}, bf16[2,2,256,256]{3,2,0,1:T(8,128)(2,1)S(1)}, u32[]{:S(2)}, u32[]{:S(2)}) collective-permute-start(bf16[2,2,256,256]{3,2,0,1:T(8,128)(2,1)S(1)} %copy.23), channel_id=1, source_target_pairs={{0,1},{1,2},{2,3},{4,5},{5,6},{6,7},{8,9},{9,10},{10,11},{12,13},{... | collective-permute-start | bytes 1572872 | tf_op jit(solution)/shard_map/ppermute | solution.py:21
  5.8 1.8 %copy.17 = bf16[4,64,2,256]{3,2,0,1:T(2,128)(2,1)} copy(bf16[4,64,2,256]{3,2,1,0:T(2,128)(2,1)} %param.9) | data formatting | bytes 524288 | tf_op args[4]
  7.7 12.4 %all-to-all-start = ((bf16[4,64,2,256]{3,2,0,1:T(2,128)(2,1)}), bf16[4,64,2,256]{3,2,0,1:T(2,128)(2,1)S(1)}, u32[]{:S(2)}, u32[]{:S(2)}) async-start(bf16[4,64,2,256]{3,2,0,1:T(2,128)(2,1)} %copy.17), calls=%async_computation | async-start | bytes 524288 | tf_op jit(solution)/shard_map/all_to_all | solution.py:474
  20.1 1.1 slice_bitcast_fusion
  21.2 0.0 collective-permute-done
  21.2 0.1 pad_maximum_fusion
  21.3 2.4 %collective-permute-start.1 = (bf16[6,256,256]{2,1,0:T(8,128)(2,1)S(1)}, bf16[6,256,256]{2,1,0:T(8,128)(2,1)S(1)}, u32[]{:S(2)}, u32[]{:S(2)}) collective-permute-start(bf16[6,256,256]{2,1,0:T(8,128)(2,1)S(1)} %pad_maximum_fusion), channel_id=1, source_target_pairs={{4,0},{8,4},{12,8},{16,12},{20,16},{24,20},{28,24},{32,28},{36,32}... | collective-permute-start | bytes 2359304 | tf_op jit(solution)/shard_map/ppermute | solution.py:21
  23.7 9.5 %all-to-all-done = bf16[4,64,2,256]{3,2,0,1:T(2,128)(2,1)S(1)} async-done(((bf16[4,64,2,256]{3,2,0,1:T(2,128)(2,1)}), bf16[4,64,2,256]{3,2,0,1:T(2,128)(2,1)S(1)}, u32[]{:S(2)}, u32[]{:S(2)}) %all-to-all-start) | async-done | bytes 262176 | tf_op jit(solution)/shard_map/all_to_all | solution.py:474
  33.2 0.1 slice.29
  33.3 0.1 copy.19
  33.4 0.1 slice.25
  33.4 1.3 %collective-permute-start.2 = (bf16[256,256]{1,0:T(8,128)(2,1)S(1)}, bf16[256,256]{1,0:T(8,128)(2,1)S(1)}, u32[]{:S(2)}, u32[]{:S(2)}) collective-permute-start(bf16[256,256]{1,0:T(8,128)(2,1)S(1)} %slice.25), channel_id=1, source_target_pairs={{1,0},{2,1},{3,2},{5,4},{6,5},{7,6},{9,8},{10,9},{11,10},{13,12},{... | collective-permute-start | bytes 393224 | tf_op jit(solution)/shard_map/ppermute | solution.py:21
  34.7 0.2 copy.18
  34.9 0.1 reshape.42
  35.1 5.1 %collective-permute-done.2 = bf16[256,256]{1,0:T(8,128)(2,1)S(1)} collective-permute-done((bf16[256,256]{1,0:T(8,128)(2,1)S(1)}, bf16[256,256]{1,0:T(8,128)(2,1)S(1)}, u32[]{:S(2)}, u32[]{:S(2)}) %collective-permute-start.2) | collective-permute-done | bytes 131104 | tf_op jit(solution)/shard_map/ppermute | solution.py:21
  40.1 0.0 copy-start
  40.1 3.4 %collective-permute-start.3 = (bf16[768,256]{1,0:T(8,128)(2,1)S(1)}, bf16[768,256]{1,0:T(8,128)(2,1)}, u32[]{:S(2)}, u32[]{:S(2)}) collective-permute-start(bf16[768,256]{1,0:T(8,128)(2,1)S(1)} %constant_dynamic-update-slice_fusion.grad), channel_id=1, source_target_pairs={{0,4},{4,8},{8,12},{12,16},{16,20},{20,24},{24,28},{28,32},{32,36}... | collective-permute-start | bytes 1179656 | tf_op jit(solution)/shard_map/ppermute | solution.py:21
  43.6 0.8 copy.20.early
  44.4 3.9 %collective-permute-done.3.grad_above = bf16[768,256]{1,0:T(8,128)(2,1)} collective-permute-done((bf16[768,256]{1,0:T(8,128)(2,1)S(1)}, bf16[768,256]{1,0:T(8,128)(2,1)}, u32[]{:S(2)}, u32[]{:S(2)}) %collective-permute-start.3) | collective-permute-done | bytes 393248 | tf_op jit(solution)/shard_map/ppermute | solution.py:21
  48.3 0.0 collective-permute-done.1.below
  48.3 0.0 copy-start.1
  48.3 0.0 copy-done
  48.3 0.9 copy-done.1
  49.2 17.7 %shard_map.92 = (bf16[512,256]{1,0:T(8,128)(2,1)}, bf16[4,2,256,256]{3,2,1,0:T(8,128)(2,1)}, bf16[2,28,256,128]{3,2,1,0:T(8,128)(2,1)}) custom-call(bf16[4,2,256,256]{3,2,1,0:T(8,128)(2,1)} %frames.1, bf16[2,2,256,256]{3,2,1,0:T(8,128)(2,1)} %copy.20.early, bf16[6,256,256]{2,1,0:T(8,128)(2,1)} %copy-done.1, f32[1,256]{1,0:T(1,128)} %bitcast.26, ...), custom_call_target="tpu_custom_call" | custom-call | flops 5500000256 | bytes 12000000 | tf_op jit(solution)/shard_map/pallas_call | solution.py:148
  66.9 1.1 reshape.43
  68.0 0.2 copy.28
  68.1 0.8 reshape.44.latent
  68.9 52.9 %shard_map.93 = (bf16[2,4,7,4,16,128]{5,4,3,2,1,0:T(8,128)(2,1)}, bf16[8,8,8,256]{3,2,1,0:T(8,128)(2,1)}) custom-call(bf16[2,28,256,128]{3,2,1,0:T(8,128)(2,1)} %get-tuple-element.12.parts, bf16[8,8,8,256]{3,2,1,0:T(8,128)(2,1)} %reshape.44.latent), custom_call_target="tpu_custom_call" | custom-call | flops 20000000 | bytes 6000000 | tf_op jit(solution)/shard_map/pallas_call | solution.py:412
  121.9 2.5 %shard_map.94 = (f32[27,64,256]{2,1,0:T(8,128)}, f32[8,256]{1,0:T(8,128)}) custom-call(bf16[2,4,7,4,16,128]{5,4,3,2,1,0:T(8,128)(2,1)} %get-tuple-element.16.total), custom_call_target="tpu_custom_call" | custom-call | tf_op jit(solution)/shard_map/pallas_call | solution.py:463
  124.4 0.8 constant_dynamic-slice_fusion
  125.2 0.5 slice_bitcast_fusion.2
  125.7 1.1 reshape.45
  126.7 0.9 copy.27
  (4 shorter events, 0.1 us)
Async XLA Ops:
  1.8 19.4 %collective-permute-start = (bf16[2,2,256,256]{3,2,0,1:T(8,128)(2,1)S(1)}, bf16[2,2,256,256]{3,2,0,1:T(8,128)(2,1)S(1)}, u32[]{:S(2)}, u32[]{:S(2)}) collective-permute-start(bf16[2,2,256,256]{3,2,0,1:T(8,128)(2,1)S(1)} %copy.23), channel_id=1, source_target_pairs={{0,1},{1,2},{2,3},{4,5},{5,6},{6,7},{8,9},{9,10},{10,11},{12,13},{... | collective-permute-start | bytes 1572872 | tf_op jit(solution)/shard_map/ppermute | solution.py:21
  7.7 25.5 %all-to-all-start = ((bf16[4,64,2,256]{3,2,0,1:T(2,128)(2,1)}), bf16[4,64,2,256]{3,2,0,1:T(2,128)(2,1)S(1)}, u32[]{:S(2)}, u32[]{:S(2)}) async-start(bf16[4,64,2,256]{3,2,0,1:T(2,128)(2,1)} %copy.17), calls=%async_computation | async-start | bytes 524288 | tf_op jit(solution)/shard_map/all_to_all | solution.py:474
  21.3 27.0 %collective-permute-start.1 = (bf16[6,256,256]{2,1,0:T(8,128)(2,1)S(1)}, bf16[6,256,256]{2,1,0:T(8,128)(2,1)S(1)}, u32[]{:S(2)}, u32[]{:S(2)}) collective-permute-start(bf16[6,256,256]{2,1,0:T(8,128)(2,1)S(1)} %pad_maximum_fusion), channel_id=1, source_target_pairs={{4,0},{8,4},{12,8},{16,12},{20,16},{24,20},{28,24},{32,28},{36,32}... | collective-permute-start | bytes 2359304 | tf_op jit(solution)/shard_map/ppermute | solution.py:21
  33.4 6.7 %collective-permute-start.2 = (bf16[256,256]{1,0:T(8,128)(2,1)S(1)}, bf16[256,256]{1,0:T(8,128)(2,1)S(1)}, u32[]{:S(2)}, u32[]{:S(2)}) collective-permute-start(bf16[256,256]{1,0:T(8,128)(2,1)S(1)} %slice.25), channel_id=1, source_target_pairs={{1,0},{2,1},{3,2},{5,4},{6,5},{7,6},{9,8},{10,9},{11,10},{13,12},{... | collective-permute-start | bytes 393224 | tf_op jit(solution)/shard_map/ppermute | solution.py:21
  40.1 8.2 %copy-start = (bf16[768,256]{1,0:T(8,128)(2,1)}, bf16[768,256]{1,0:T(8,128)(2,1)S(1)}, u32[]{:S(2)}) copy-start(bf16[768,256]{1,0:T(8,128)(2,1)S(1)} %constant_dynamic-update-slice_fusion.grad) | copy-start | bytes 1179652
  40.1 8.1 %collective-permute-start.3 = (bf16[768,256]{1,0:T(8,128)(2,1)S(1)}, bf16[768,256]{1,0:T(8,128)(2,1)}, u32[]{:S(2)}, u32[]{:S(2)}) collective-permute-start(bf16[768,256]{1,0:T(8,128)(2,1)S(1)} %constant_dynamic-update-slice_fusion.grad), channel_id=1, source_target_pairs={{0,4},{4,8},{8,12},{12,16},{16,20},{20,24},{24,28},{28,32},{32,36}... | collective-permute-start | bytes 1179656 | tf_op jit(solution)/shard_map/ppermute | solution.py:21
  48.3 0.9 copy-start.1

commit v2 on v1

--- a/solution.py
+++ b/solution.py
@@ -1,5 +1,3 @@
-import functools
-
 import jax
 import jax.numpy as jnp
 from jax import lax
@@ -13,12 +11,6 @@
 EPS = 1e-06
 NX, NZ, NY = 4, 8, 4
 CHUNKS, TAPS = 7, 4
-
-
-def shifted(value, axis, steps):
-    count = lax.axis_size(axis)
-    leading, last = (max(0, -steps), min(count, count - steps))
-    return lax.ppermute(value, axis, [(source, source + steps) for source in range(leading, last)])
 
 
 def dot_nt(left, right):
@@ -468,13 +460,178 @@
     )(total)
 
 
+def gather_kernel(
+    blocks, frames, grad, grad_above, early, below,
+    middle, landed, flat, woven, z_sem, slab_sem, near_sem,
+):
+    rows_at = lax.axis_index("rows")
+    y = lax.axis_index("tm")
+    slab, z = rows_at % (2 * NX), rows_at // (2 * NX)
+    count = NZ * 2 * NX
+
+    def along(axis, step):
+        if axis == "y":
+            return (rows_at, (y + step + NY) % NY)
+        if axis == "slab":
+            return (z * (2 * NX) + (slab + step) % (2 * NX), y)
+        if axis == "row":
+            return ((rows_at + step + count) % count, y)
+        return (((z + step) % NZ) * (2 * NX) + slab, y)
+
+    barrier = pltpu.get_barrier_semaphore()
+    friends = [along("z", step) for step in range(1, NZ)] + [along("slab", step) for step in range(1, 2 * NX)]
+    friends += [along("y", 1), along("y", -1), along("row", 1), along("row", -1)]
+    for friend in friends:
+        pl.semaphore_signal(barrier, inc=1, device_id=friend, device_id_type=MESH)
+    pl.semaphore_wait(barrier, len(friends))
+
+    def copy_to(source, target, sems, at, device):
+        return pltpu.make_async_remote_copy(
+            src_ref=source, dst_ref=target, send_sem=sems.at[0, at], recv_sem=sems.at[1, at],
+            device_id=device, device_id_type=MESH,
+        )
+
+    outer = [
+        copy_to(blocks.at[(z + step) % NZ], middle.at[z], z_sem, step, along("z", step)) for step in range(1, NZ)
+    ]
+    inner = [
+        copy_to(middle.at[:, (slab + step) % (2 * NX)], landed.at[:, slab], slab_sem, step, along("slab", step))
+        for step in range(1, 2 * NX)
+    ]
+    early_on = copy_to(frames.at[pl.ds(2, 2)], early, near_sem, 0, along("y", 1))
+    below_own = copy_to(frames.at[:, 0], below.at[pl.ds(2, 4)], near_sem, 1, along("row", -1))
+    below_early = copy_to(early.at[:, 0], below.at[pl.ds(0, 2)], near_sem, 2, along("row", -1))
+    ahead, own, late = pl.ds(0, 256), pl.ds(0, 512), pl.ds(512, 256)
+    grad_late = copy_to(grad.at[ahead], grad.at[late], near_sem, 3, along("y", -1))
+    above_own = copy_to(grad.at[own], grad_above.at[own], near_sem, 4, along("row", 1))
+    above_late = copy_to(grad.at[late], grad_above.at[late], near_sem, 5, along("row", 1))
+    first_time, last_time, first_row, last_row = y == 0, y == NY - 1, rows_at == 0, rows_at == count - 1
+
+    for copy in outer:
+        copy.start()
+
+    @pl.when(jnp.logical_not(last_time))
+    def _():
+        early_on.start()
+
+    @pl.when(jnp.logical_not(first_row))
+    def _():
+        below_own.start()
+
+    middle[z] = blocks[z]
+
+    @pl.when(first_time)
+    def _():
+        early[...] = jnp.zeros_like(early)
+
+    @pl.when(last_row)
+    def _():
+        below[...] = jnp.zeros_like(below)
+
+    @pl.when(first_row)
+    def _():
+        grad_above[...] = jnp.zeros_like(grad_above)
+
+    @pl.when(last_time)
+    def _():
+        grad[late, :] = jnp.zeros((256, 256), BF16)
+
+    for copy in outer:
+        copy.wait_recv()
+    for copy in inner:
+        copy.start()
+    landed[:, slab] = middle[:, slab]
+    for copy in inner:
+        copy.wait_recv()
+
+    for half in range(2):
+        lanes = pl.ds(half * 128, 128)
+        flat[half] = landed[:, :, :, lanes].astype(F32).reshape(512, 128)
+    for frame in range(4):
+        for half in range(2):
+            for side in range(2):
+                woven[frame, half, pl.ds(side, 64, stride=2), :] = flat[half, pl.ds(2 * frame + side, 64, stride=8), :]
+            grad[pl.ds(frame * 128, 128), pl.ds(half * 128, 128)] = woven[frame, half].astype(BF16)
+
+    @pl.when(jnp.logical_not(first_time))
+    def _():
+        grad_late.start()
+
+    @pl.when(jnp.logical_not(last_row))
+    def _():
+        above_own.start()
+
+    @pl.when(jnp.logical_not(first_time))
+    def _():
+        early_on.wait_recv()
+
+    @pl.when(jnp.logical_not(first_row))
+    def _():
+        below_early.start()
+
+    @pl.when(jnp.logical_not(last_time))
+    def _():
+        grad_late.wait_recv()
+
+    @pl.when(jnp.logical_not(last_row))
+    def _():
+        above_late.start()
+
+    @pl.when(jnp.logical_not(first_row))
+    def _():
+        above_own.wait_recv()
+        above_late.wait_recv()
+        below_own.wait_send()
+        below_early.wait_send()
+
+    @pl.when(jnp.logical_not(last_row))
+    def _():
+        below_own.wait_recv()
+        below_early.wait_recv()
+        above_own.wait_send()
+        above_late.wait_send()
+
+    @pl.when(jnp.logical_not(first_time))
+    def _():
+        grad_late.wait_send()
+
+    @pl.when(jnp.logical_not(last_time))
+    def _():
+        early_on.wait_send()
+
+    for copy in outer + inner:
+        copy.wait_send()
+
+
+def gather(blocks, frames):
+    dma = pltpu.SemaphoreType.DMA
+    return pl.pallas_call(
+        gather_kernel,
+        out_shape=(
+            jax.ShapeDtypeStruct((768, 256), BF16),
+            jax.ShapeDtypeStruct((768, 256), BF16),
+            jax.ShapeDtypeStruct((2, 2, 256, 256), BF16),
+            jax.ShapeDtypeStruct((6, 256, 256), BF16),
+        ),
+        in_specs=[pl.BlockSpec(memory_space=pltpu.VMEM)] * 2,
+        out_specs=[pl.BlockSpec(memory_space=pltpu.VMEM)] * 4,
+        scratch_shapes=[
+            pltpu.VMEM((NZ, 2 * NX, 8, 256), BF16),
+            pltpu.VMEM((NZ, 2 * NX, 8, 256), BF16),
+            pltpu.VMEM((2, 512, 128), F32),
+            pltpu.VMEM((4, 2, 128, 128), F32),
+            dma((2, NZ)),
+            dma((2, 2 * NX)),
+            dma((2, 6)),
+        ],
+        compiler_params=pltpu.CompilerParams(collective_id=2, has_side_effects=True),
+        cost_estimate=pl.CostEstimate(flops=1_000_000, bytes_accessed=4_000_000, transcendentals=0),
+    )(blocks, frames)
+
+
 def on_device(frames, norm_gain, conv_weight, conv_bias, latent_grad):
-    early = shifted(frames[2:], "tm", 1)
-    below = shifted(jnp.concatenate([early[:, 0], frames[:, 0]], axis=0), "rows", -1)
-    grad_rows = lax.all_to_all(latent_grad, "rows", split_axis=1, concat_axis=2, tiled=True)
-    grad_rows = grad_rows.reshape(512, 256)
-    grad = jnp.concatenate([grad_rows, shifted(grad_rows[:256], "tm", -1)], axis=0)
-    grad_above = shifted(grad, "rows", 1)
+    blocks = latent_grad.transpose(1, 0, 2, 3).reshape(NZ, 2 * NX, 8, 256)
+    grad, grad_above, early, below = gather(blocks, frames)
     latent_rows, frames_grad, parts = section(
         frames, early, below, norm_gain.reshape(1, 256), conv_weight.reshape(3, 9, 256, 256),
         conv_bias.reshape(1, 256), grad, grad_above,

time: 128 us -> 117 us (0.914)
  Pallas kernels: 73.2 us -> 109 us
  starting transfers between devices: 23.6 us -> 0 us
  waiting for transfers between devices: 18.4 us -> 0 us
  local copies, waits for them, and re-layouts: 11.6 us -> 7.18 us
    pallas_call x0 -> x1, Pallas kernels: none -> 31.1 us  [gather(): pl.pallas_call(gather_kernel, out_shape=(jax.ShapeDtypeStruct((768, 256),...]
    all_to_all x1 -> x0, starting transfers between devices: 12.4 us -> none  [on_device(): lax.all_to_all(latent_grad, 'rows', split_axis=1, concat_axis=2, tiled=True)]
    ppermute x4 -> x0, starting transfers between devices: 11.1 us -> none  [shifted(): lax.ppermute(value, axis, [(source, source + steps) for source in range(l...]
    all_to_all x1 -> x0, waiting for transfers between devices: 9.5 us -> none  [on_device(): lax.all_to_all(latent_grad, 'rows', split_axis=1, concat_axis=2, tiled=True)]
    ppermute x4 -> x0, waiting for transfers between devices: 8.92 us -> none  [shifted(): lax.ppermute(value, axis, [(source, source + steps) for source in range(l...]
    pallas_call x1, Pallas kernels: 52.9 us -> 57.7 us  [reduce_all(): pl.pallas_call(reduce_kernel, out_shape=(jax.ShapeDtypeStruct((2, NX, CHU...]
    unnamed x7 -> x0, local copies, waits for them, and re-layouts: 2.77 us -> none
    slice x4 -> x0, local copies, waits for them, and re-layouts: 1.32 us -> none  [the longest x1 1.08 us: on_device(): early = shifted(frames[2:], 'tm', 1)]
  transfers between devices with their start and end apart: 5 -> 0, of which waited for: 3 -> 0; matrix products, arithmetic and copies ran while one was open for 3% -> 0% of each run, Pallas kernels for 0% -> 0%
where the time goes in v2:
time: 117 us
  Pallas kernels  109 us (93%)
  local copies, waits for them, and re-layouts  7.18 us (6%)
    pallas_call x1, Pallas kernels, reduce_all(): pl.pallas_call(reduce_kernel, out_shape=(jax.ShapeDtypeStruct((2, NX, CHU...  57.7 us
    pallas_call x1, Pallas kernels, gather(): pl.pallas_call(gather_kernel, out_shape=(jax.ShapeDtypeStruct((768, 256),...  31.1 us
    pallas_call x1, Pallas kernels, section(): pl.pallas_call(section_kernel, out_shape=(jax.ShapeDtypeStruct((512, 256)...  17.7 us
    pallas_call x1, Pallas kernels, finish(): pl.pallas_call(finish_kernel, out_shape=(jax.ShapeDtypeStruct((27, 64, 25...  2.51 us

profile of v2, /device:TPU:1, one launch (start us, length us, event | category | flops | bytes accessed | tf_op | source)
XLA Modules:
  0.0 116.9 jit_solution(14567595548173809433)
XLA Ops:
  0.6 1.1 copy.10
  1.8 0.8 reshape.34.blocks
  2.6 31.1 %shard_map.92 = (bf16[768,256]{1,0:T(8,128)(2,1)}, bf16[768,256]{1,0:T(8,128)(2,1)}, bf16[2,2,256,256]{3,2,1,0:T(8,128)(2,1)}, bf16[6,256,256]{2,1,0:T(8,128)(2,1)}) custom-call(bf16[8,8,8,256]{3,2,1,0:T(8,128)(2,1)} %reshape.34.blocks, bf16[4,2,256,256]{3,2,1,0:T(8,128)(2,1)} %frames.3), custom_call_target="tpu_custom_call" | custom-call | flops 1000000 | bytes 4000000 | tf_op jit(solution)/shard_map/pallas_call | solution.py:608
  33.6 17.7 %shard_map.93 = (bf16[512,256]{1,0:T(8,128)(2,1)}, bf16[4,2,256,256]{3,2,1,0:T(8,128)(2,1)}, bf16[2,28,256,128]{3,2,1,0:T(8,128)(2,1)}) custom-call(bf16[4,2,256,256]{3,2,1,0:T(8,128)(2,1)} %frames.3, bf16[2,2,256,256]{3,2,1,0:T(8,128)(2,1)} %get-tuple-element.16.early, bf16[6,256,256]{2,1,0:T(8,128)(2,1)} %get-tuple-element.17.below, f32[1,256]{1,0:T(1,128)} %bitcast.22, ...), custom_call_target="tpu_custom_call" | custom-call | flops 5500000256 | bytes 12000000 | tf_op jit(solution)/shard_map/pallas_call | solution.py:140
  51.4 1.1 reshape.38
  52.4 0.2 copy.16
  52.6 0.8 reshape.39.latent
  53.4 57.7 %shard_map.94 = (bf16[2,4,7,4,16,128]{5,4,3,2,1,0:T(8,128)(2,1)}, bf16[8,8,8,256]{3,2,1,0:T(8,128)(2,1)}) custom-call(bf16[2,28,256,128]{3,2,1,0:T(8,128)(2,1)} %get-tuple-element.20.parts, bf16[8,8,8,256]{3,2,1,0:T(8,128)(2,1)} %reshape.39.latent), custom_call_target="tpu_custom_call" | custom-call | flops 20000000 | bytes 6000000 | tf_op jit(solution)/shard_map/pallas_call | solution.py:404
  111.2 2.5 %shard_map.95 = (f32[27,64,256]{2,1,0:T(8,128)}, f32[8,256]{1,0:T(8,128)}) custom-call(bf16[2,4,7,4,16,128]{5,4,3,2,1,0:T(8,128)(2,1)} %get-tuple-element.24.total), custom_call_target="tpu_custom_call" | custom-call | tf_op jit(solution)/shard_map/pallas_call | solution.py:455
  113.7 0.8 constant_dynamic-slice_fusion
  114.5 0.5 slice_bitcast_fusion
  115.0 1.1 reshape.40
  116.0 0.9 copy.15

commit v3 on v1

v3 whole, which is shorter than its diff:
```python
import jax
import jax.numpy as jnp
from jax import lax
from jax.experimental import pallas as pl
from jax.experimental.pallas import tpu as pltpu
from jax.sharding import PartitionSpec as P

F32 = jnp.float32
BF16 = jnp.bfloat16
MESH = pl.DeviceIdType.MESH
EPS = 1e-06
NX, NZ, NY = 4, 8, 4
CHUNKS, TAPS = 7, 4


def dot_nt(left, right):
    return lax.dot_general(left, right, (((1,), (1,)), ((), ())), preferred_element_type=F32)


def dot_nn(left, right):
    return lax.dot_general(left, right, (((1,), (0,)), ((), ())), preferred_element_type=F32)


def inverse_rms(signal):
    return lax.rsqrt(jnp.mean(signal * signal, axis=-1, keepdims=True) + EPS)


def whole_kernel(
    latent_grad, frames, gain, weight_far, bias,
    frames_grad, latent, result,
    weight, blocks, middle, landed, flat, woven, grad, grad_above, early, below,
    columns, turned, grad_next, spread, tile, gain_sum, parts,
    other, mine, first_plus, first_minus, second_plus, second_minus,
    mid, first_plus2, first_minus2, second_plus2, second_minus2,
    low, arrive, total, block, latent_in, latent_mid, latent_out,
    weight_sem, gz_sem, gs_sem, near_sem,
    core_sem, ring_sem, ring2_sem, z_sem, zback_sem, x_sem, pair_sem, lat_sem,
):
    rows_at = lax.axis_index("rows")
    y = lax.axis_index("tm")
    core, x, z = rows_at % 2, (rows_at // 2) % NX, rows_at // (2 * NX)
    slab = rows_at % (2 * NX)
    count = NZ * 2 * NX

    def row_of(z_at, x_at, core_at):
        return z_at * (2 * NX) + x_at * 2 + core_at

    sibling = (row_of(z, x, 1 - core), y)

    def along(axis, step):
        if axis == "y":
            return (rows_at, (y + step + NY) % NY)
        if axis == "x":
            return (row_of(z, (x + step) % NX, core), y)
        if axis == "slab":
            return (z * (2 * NX) + (slab + step) % (2 * NX), y)
        if axis == "row":
            return ((rows_at + step + count) % count, y)
        return (row_of((z + step) % NZ, x, core), y)

    weight_in = pltpu.make_async_copy(weight_far, weight, weight_sem.at[0])
    weight_in.start()

    barrier = pltpu.get_barrier_semaphore()
    friends = [along("z", step) for step in range(1, NZ)] + [along("slab", step) for step in range(1, 2 * NX)]
    friends += [along("y", 1), along("y", -1), along("row", 1), along("row", -1)]
    for friend in friends:
        pl.semaphore_signal(barrier, inc=1, device_id=friend, device_id_type=MESH)

    def unweave(target):
        for frame in range(4):
            for half in range(2):
                for side in range(2):
                    flat[half, pl.ds(2 * frame + side, 64, stride=8), :] = woven[frame, half, pl.ds(side, 64, stride=2), :]
        for half in range(2):
            target[:, :, :, pl.ds(half * 128, 128)] = flat[half].reshape(NZ, 2 * NX, 8, 128).astype(BF16)

    def weave(source, put):
        for half in range(2):
            flat[half] = source[:, :, :, pl.ds(half * 128, 128)].astype(F32).reshape(512, 128)
        for frame in range(4):
            for half in range(2):
                for side in range(2):
                    woven[frame, half, pl.ds(side, 64, stride=2), :] = flat[half, pl.ds(2 * frame + side, 64, stride=8), :]
                put(frame, half, woven[frame, half].astype(BF16))

    for frame in range(4):
        for half in range(2):
            woven[frame, half] = latent_grad[frame, :, pl.ds(half * 128, 128)].astype(F32)
    unweave(blocks)

    pl.semaphore_wait(barrier, len(friends))

    def copy_to(source, target, sems, at, device):
        return pltpu.make_async_remote_copy(
            src_ref=source, dst_ref=target, send_sem=sems.at[(0, *at)], recv_sem=sems.at[(1, *at)],
            device_id=device, device_id_type=MESH,
        )

    def send(*args):
        copy = copy_to(*args)
        copy.start()
        return copy

    ahead, own, late = pl.ds(0, 256), pl.ds(0, 512), pl.ds(512, 256)
    early_on = copy_to(frames.at[pl.ds(2, 2)], early, near_sem, (0,), along("y", 1))
    below_own = copy_to(frames.at[:, 0], below.at[pl.ds(2, 4)], near_sem, (1,), along("row", -1))
    below_early = copy_to(early.at[:, 0], below.at[pl.ds(0, 2)], near_sem, (2,), along("row", -1))
    grad_late = copy_to(grad.at[ahead], grad.at[late], near_sem, (3,), along("y", -1))
    above_own = copy_to(grad.at[own], grad_above.at[own], near_sem, (4,), along("row", 1))
    above_late = copy_to(grad.at[late], grad_above.at[late], near_sem, (5,), along("row", 1))
    has_past, has_future = y > 0, y < NY - 1
    has_above, has_below = rows_at > 0, rows_at < count - 1

    def only(condition, *actions):
        @pl.when(condition)
        def _():
            for action in actions:
                action()

    g_outer = [
        send(blocks.at[(z + step) % NZ], middle.at[z], gz_sem, (step,), along("z", step)) for step in range(1, NZ)
    ]
    only(has_future, early_on.start)
    only(has_above, below_own.start)
    middle[z] = blocks[z]

    @pl.when(jnp.logical_not(has_past))
    def _():
        early[...] = jnp.zeros_like(early)

    @pl.when(jnp.logical_not(has_below))
    def _():
        below[...] = jnp.zeros_like(below)

    @pl.when(jnp.logical_not(has_above))
    def _():
        grad_above[...] = jnp.zeros_like(grad_above)

    @pl.when(jnp.logical_not(has_future))
    def _():
        grad[late, :] = jnp.zeros((256, 256), BF16)

    gain_row = gain[...]
    row_at = lax.broadcasted_iota(jnp.int32, (128, 256), 0)

    def hidden_tile(source, at, row, keep):
        for piece_at in range(4):
            rows = pl.ds(piece_at * 64, 64)
            signal = source[rows, :].astype(F32)
            normed = signal * inverse_rms(signal) * gain_row
            hidden = normed / (1.0 + jnp.exp(-normed))
            tile[row, 0, rows, :] = hidden[:, :128]
            tile[row, 1, rows, :] = hidden[:, 128:]
        even = jnp.concatenate([tile[row, half, pl.ds(0, 128, stride=2), :] for half in range(2)], axis=1)
        odd = jnp.concatenate([tile[row, half, pl.ds(1, 128, stride=2), :] for half in range(2)], axis=1)
        after = jnp.where(row_at == 127, 0.0, pltpu.roll(even, 127, 0))
        where = pl.ds(pl.multiple_of(at * 128, 128), 128)
        columns[where, pl.ds(row * 768, 256)] = even.astype(BF16)
        columns[where, pl.ds(row * 768 + 256, 256)] = odd.astype(BF16)
        columns[where, pl.ds(row * 768 + 512, 256)] = after.astype(BF16)
        if keep:
            lanes = pl.ds(pl.multiple_of((at - 2) * 128, 128), 128)
            turned[2 * row, :, lanes] = even.T.astype(BF16)
            turned[2 * row + 1, :, lanes] = odd.T.astype(BF16)

    @pl.loop(2, 6)
    def _(at):
        hidden_tile(frames.at[at - 2, 0], at, 0, True)
        hidden_tile(frames.at[at - 2, 1], at, 1, True)

    for copy in g_outer:
        copy.wait_recv()
    g_inner = [
        send(middle.at[:, (slab + step) % (2 * NX)], landed.at[:, slab], gs_sem, (step,), along("slab", step))
        for step in range(1, 2 * NX)
    ]
    landed[:, slab] = middle[:, slab]
    spread[...] = jnp.zeros_like(spread)
    gain_sum[...] = jnp.zeros_like(gain_sum)
    weight_in.wait()
    for copy in g_inner:
        copy.wait_recv()

    def put_grad(frame, half, value):
        grad[pl.ds(frame * 128, 128), pl.ds(half * 128, 128)] = value

    weave(landed, put_grad)
    only(has_past, grad_late.start)
    only(has_below, above_own.start)

    def step_on(which, source, frames_at):
        for at in frames_at:
            where = pl.ds(at * 128, 128)
            moved = pltpu.roll(source[where, :].astype(F32), 1, 0)
            grad_next[which, where, :] = jnp.where(row_at == 0, 0.0, moved).astype(BF16)

    def weight_taps(chunk):
        for tap in range(chunk * TAPS, min(27, chunk * TAPS + TAPS)):
            tap_t, tap_r, tap_c = tap // 9, tap // 3 % 3, tap % 3
            where = pl.ds((2 - tap_t) * 128, 512)
            left = turned[2 * (tap_r % 2) + tap_c % 2]
            if tap_c == 2:
                right = grad_next[1 if tap_r == 2 else 0, where, :]
            else:
                right = (grad_above if tap_r == 2 else grad)[where, :]
            product = dot_nn(left, right).astype(BF16)
            parts[0, tap] = product[:, :128]
            parts[1, tap] = product[:, 128:]

    pair = {}

    def pair_send(chunk):
        spots = pl.ds(chunk * TAPS, TAPS)
        pair[chunk] = send(parts.at[1 - core, spots], other.at[spots], core_sem, (chunk,), sibling)

    def axes_of(chunk):
        return ("y", "x") if chunk % 2 == 0 else ("x", "y")

    def here(axis, step):
        return (y + step) % NY if axis == "y" else (x + step) % NX

    def piece(ref, chunk, stage, at, taps):
        if stage == 0 and axes_of(chunk)[0] == "x":
            return ref.at[chunk, taps, slice(None), at]
        return ref.at[chunk, taps, at]

    FIRST, LAST, ALL = pl.ds(0, 2), pl.ds(2, 2), pl.ds(0, 4)
    banks = (
        (mine, first_plus, first_minus, second_plus, second_minus, ring_sem, BF16),
        (mid, first_plus2, first_minus2, second_plus2, second_minus2, ring2_sem, F32),
    )

    def ring_open(chunk, stage):
        source, plus, minus, _, _, sems, _ = banks[stage]
        axis = axes_of(chunk)[stage]
        far = here(axis, 2)
        return [
            send(piece(source, chunk, stage, far, FIRST), plus.at[chunk], sems, (chunk, 0), along(axis, 1)),
            send(piece(source, chunk, stage, far, LAST), minus.at[chunk], sems, (chunk, 1), along(axis, 3)),
        ]

    def ring_next(chunk, stage, opened):
        source, plus, minus, plus_in, minus_in, sems, kind = banks[stage]
        axis = axes_of(chunk)[stage]
        opened[0].wait_recv()
        ahead = piece(source, chunk, stage, here(axis, 1), FIRST)
        ahead[...] = (ahead[...].astype(F32) + plus[chunk].astype(F32)).astype(kind)
        one = send(piece(source, chunk, stage, here(axis, 1), ALL), plus_in.at[chunk], sems, (chunk, 2), along(axis, 1))
        opened[1].wait_recv()
        behind = piece(source, chunk, stage, here(axis, 3), LAST)
        behind[...] = (behind[...].astype(F32) + minus[chunk].astype(F32)).astype(kind)
        two = send(piece(source, chunk, stage, here(axis, 3), ALL), minus_in.at[chunk], sems, (chunk, 3), along(axis, 3))
        return [one, two]

    def ring_close(chunk, stage, sent):
        source, _, _, plus_in, minus_in, _, _ = banks[stage]
        axis = axes_of(chunk)[stage]
        sent[0].wait_recv()
        sent[1].wait_recv()
        own = piece(source, chunk, stage, here(axis, 0), ALL)[...].astype(F32)
        (mid, low)[stage][chunk] = own + plus_in[chunk].astype(F32) + minus_in[chunk].astype(F32)

    def to_owner(chunk):
        step = (chunk - z + NZ) % NZ
        return pltpu.make_async_remote_copy(
            src_ref=low.at[chunk], dst_ref=arrive.at[step], send_sem=z_sem.at[0, chunk], recv_sem=z_sem.at[1, step],
            device_id=(row_of(chunk, x, core), y), device_id_type=MESH,
        )

    opened, sent, opened2, sent2 = {}, {}, {}, {}

    def pair_close(chunk):
        pair[chunk].wait_recv()
        spots = pl.ds(chunk * TAPS, TAPS)
        summed = parts[core, spots].astype(F32) + other[spots].astype(F32)
        mine[chunk] = summed.astype(BF16).reshape(TAPS, NY, NX, 16, 128)
        opened[chunk] = ring_open(chunk, 0)

    def next_one(*chunks):
        for chunk in chunks:
            sent[chunk] = ring_next(chunk, 0, opened[chunk])

    def close_one(*chunks):
        for chunk in chunks:
            ring_close(chunk, 0, sent[chunk])
            opened2[chunk] = ring_open(chunk, 1)

    def next_two(*chunks):
        for chunk in chunks:
            sent2[chunk] = ring_next(chunk, 1, opened2[chunk])

    def close_two(*chunks):
        for chunk in chunks:
            ring_close(chunk, 1, sent2[chunk])
            only(z != chunk, to_owner(chunk).start)

    step_on(0, grad, range(4))
    weight_taps(5)
    pair_send(5)
    only(has_future, grad_late.wait_recv)
    only(has_below, above_late.start)
    step_on(0, grad, (4, 5))
    weight_taps(0)
    pair_send(0)
    pair_close(5)
    only(has_above, above_own.wait_recv, above_late.wait_recv)
    step_on(1, grad_above, range(6))
    before = 0
    for chunk in (3, 1, 2, 4):
        weight_taps(chunk)
        pair_send(chunk)
        pair_close(before)
        before = chunk
    only(has_past, early_on.wait_recv)
    only(has_above, below_early.start)

    def back_taps(tap):
        where = pl.ds((2 - tap) * 128, 512)
        here_g, here_next = grad[where, :], grad_next[0, where, :]
        above, above_next = grad_above[where, :], grad_next[1, where, :]
        spread[0] += dot_nt(here_g, weight[tap, 0]) + dot_nt(here_next, weight[tap, 2])
        spread[0] += dot_nt(above, weight[tap, 6]) + dot_nt(above_next, weight[tap, 8])
        spread[1] += dot_nt(here_g, weight[tap, 1]) + dot_nt(above, weight[tap, 7])
        spread[2] += dot_nt(here_g, weight[tap, 3]) + dot_nt(here_next, weight[tap, 5])
        spread[3] += dot_nt(here_g, weight[tap, 4])

    def frame_back(first, last):
        @pl.loop(first, last)
        def _(at):
            where = pl.ds(pl.multiple_of(at * 128, 128), 128)
            for row in range(2):
                for half in range(2):
                    lanes = pl.ds(half * 128, 128)
                    tile[row, half, pl.ds(0, 128, stride=2), :] = spread[2 * row, where, lanes]
                    tile[row, half, pl.ds(1, 128, stride=2), :] = spread[2 * row + 1, where, lanes]
                for piece_at in range(4):
                    rows = pl.ds(piece_at * 64, 64)
                    signal = frames[at, row, rows, :].astype(F32)
                    inv = inverse_rms(signal)
                    unit = signal * inv
                    normed = unit * gain_row
                    sigma = 1.0 / (1.0 + jnp.exp(-normed))
                    arrived = jnp.concatenate([tile[row, half, rows, :] for half in range(2)], axis=1)
                    normed_grad = arrived * sigma * (1.0 + normed * (1.0 - sigma))
                    gain_sum[...] += jnp.sum((normed_grad * unit).reshape(8, 8, 256), axis=0)
                    unit_grad = normed_grad * gain_row
                    mean = jnp.mean(unit_grad * unit, axis=-1, keepdims=True)
                    frames_grad[at, row, rows, :] = (inv * (unit_grad - unit * mean)).astype(BF16)

    back_taps(0)
    pair_close(before)
    next_one(5, 0)
    back_taps(1)
    next_one(3, 1)
    back_taps(2)
    next_one(2, 4)
    frame_back(0, 2)
    close_one(5, 0)
    frame_back(2, 4)

    gain_local = jnp.sum(gain_sum[...], axis=0, keepdims=True)
    bias_local = jnp.sum(grad[pl.ds(0, 512), :].astype(F32), axis=0, keepdims=True)
    gain_rest = gain_local - gain_local.astype(BF16).astype(F32)
    bias_rest = bias_local - bias_local.astype(BF16).astype(F32)
    spot = lax.broadcasted_iota(jnp.int32, (256, 256), 0) % 64
    small = jnp.where(spot == 0, gain_local, jnp.where(spot == 1, bias_local, 0.0))
    small = jnp.where(spot == 2, gain_rest, jnp.where(spot == 3, bias_rest, small)).astype(BF16)
    parts[0, 27] = small[:, :128]
    parts[1, 27] = small[:, 128:]
    weight_taps(6)
    pair_send(6)
    close_one(3, 1)

    @pl.loop(0, 2)
    def _(at):
        hidden_tile(early.at[at, 0], at, 0, False)
        hidden_tile(early.at[at, 1], at, 1, False)

    pair_close(6)
    close_one(2, 4)
    next_two(5, 0)
    only(has_below, below_own.wait_recv, below_early.wait_recv)

    @pl.loop(0, 6)
    def _(at):
        hidden_tile(below.at[at], at, 2, False)

    next_one(6)
    next_two(3, 1)
    spread[0] = jnp.broadcast_to(bias[...], (512, 256))

    @pl.loop(0, 3)
    def _(tap):
        where = pl.ds(pl.multiple_of(tap * 128, 128), 512)
        spread[0] += dot_nn(columns[where, :], weight[tap].reshape(2304, 256))

    next_two(2, 4)
    close_one(6)
    close_two(5, 0, 3, 1)
    for frame in range(4):
        for half in range(2):
            woven[frame, half] = spread[0, pl.ds(frame * 128, 128), pl.ds(half * 128, 128)]
    unweave(latent_in)
    outer = [
        send(latent_in.at[(z + step) % NZ], latent_mid.at[z], lat_sem, (0, step), along("z", step))
        for step in range(1, NZ)
    ]
    latent_mid[z] = latent_in[z]
    next_two(6)
    close_two(2, 4, 6)
    started = list(pair.values()) + outer + g_outer + g_inner
    for table in (opened, sent, opened2, sent2):
        for chunk in range(CHUNKS):
            started += table[chunk]

    def back(step):
        return copy_to(total.at[z], total.at[z], zback_sem, (step,), along("z", step))

    @pl.when(z < CHUNKS)
    def _():
        summed = low[z]
        for step in range(1, NZ):
            pltpu.make_async_remote_copy(
                src_ref=low.at[0], dst_ref=arrive.at[step], send_sem=z_sem.at[0, 0], recv_sem=z_sem.at[1, step],
                device_id=sibling, device_id_type=MESH,
            ).wait_recv()
            summed += arrive[step]
        total[z] = summed.astype(BF16)
        for step in range(1, NZ):
            back(step).start()

    right, left, across = (x + 1) % NX, (x + 3) % NX, (x + 2) % NX
    order = (0, 1, 7, 2, 6, 3, 5, 4)

    def to_right(step, at):
        return copy_to(total.at[at], block.at[x, at], x_sem, (0, step), along("x", 1))

    def to_left(step, at):
        return copy_to(total.at[at], block.at[x, at], x_sem, (1, step), along("x", 3))

    def on_right(step, at):
        half = block.at[left, at, FIRST]
        return copy_to(half, half, x_sem, (2, step), along("x", 1))

    def on_left(step, at):
        half = block.at[right, at, LAST]
        return copy_to(half, half, x_sem, (3, step), along("x", 3))

    def across_core(which, step, at):
        source = total.at[at] if which == 0 else block.at[(left, right, across)[which - 1], at]
        where = (x, left, right, across)[which]
        return copy_to(source, result.at[core, where, at], pair_sem, (which, step), sibling)

    def each(body):
        for step in order:
            at = (z - step + NZ) % NZ

            @pl.when(at < CHUNKS)
            def _():
                body(step, at)

    def fan_one(step, at):
        if step:
            back(step).wait_recv()
        to_right(step, at).start()
        to_left(step, at).start()
        across_core(0, step, at).start()
        result[core, x, at] = total[at]

    def fan_two(step, at):
        to_right(step, at).wait_recv()
        on_right(step, at).start()
        across_core(1, step, at).start()
        result[core, left, at] = block[left, at]
        to_left(step, at).wait_recv()
        on_left(step, at).start()
        across_core(2, step, at).start()
        result[core, right, at] = block[right, at]

    def fan_three(step, at):
        on_right(step, at).wait_recv()
        on_left(step, at).wait_recv()
        across_core(3, step, at).start()
        result[core, across, at] = block[across, at]

    def fan_last(step, at):
        for which in range(4):
            across_core(which, step, at).wait()
        to_right(step, at).wait_send()
        to_left(step, at).wait_send()
        on_right(step, at).wait_send()
        on_left(step, at).wait_send()

    for copy in outer:
        copy.wait_recv()
    inner = [
        send(latent_mid.at[:, (slab + step) % (2 * NX)], latent_out.at[:, slab], lat_sem, (1, step), along("slab", step))
        for step in range(1, 2 * NX)
    ]
    latent_out[:, slab] = latent_mid[:, slab]
    each(fan_one)
    each(fan_two)
    for copy in inner:
        copy.wait_recv()

    def put_latent(frame, half, value):
        latent[frame, :, pl.ds(half * 128, 128)] = value

    weave(latent_out, put_latent)
    each(fan_three)
    for copy in started + inner:
        copy.wait_send()
    each(fan_last)
    only(has_future, early_on.wait_send)
    only(has_above, below_own.wait_send, below_early.wait_send)
    only(has_past, grad_late.wait_send)
    only(has_below, above_own.wait_send, above_late.wait_send)
    for chunk in range(CHUNKS):
        only(z != chunk, to_owner(chunk).wait_send)

    @pl.when(z < CHUNKS)
    def _():
        for step in range(1, NZ):
            back(step).wait_send()


def whole(latent_grad, frames, gain, weight, bias):
    dma, vmem = pltpu.SemaphoreType.DMA, pltpu.VMEM
    inside = pl.BlockSpec(memory_space=pltpu.VMEM)
    return pl.pallas_call(
        whole_kernel,
        out_shape=(
            jax.ShapeDtypeStruct((4, 2, 256, 256), BF16),
            jax.ShapeDtypeStruct((4, 128, 256), BF16),
            jax.ShapeDtypeStruct((2, NX, CHUNKS, TAPS, 16, 128), BF16),
        ),
        in_specs=[inside, inside, inside, pl.BlockSpec(memory_space=pl.ANY), inside],
        out_specs=[inside] * 3,
        scratch_shapes=[
            vmem((3, 9, 256, 256), BF16),
            vmem((NZ, 2 * NX, 8, 256), BF16),
            vmem((NZ, 2 * NX, 8, 256), BF16),
            vmem((NZ, 2 * NX, 8, 256), BF16),
            vmem((2, 512, 128), F32),
            vmem((4, 2, 128, 128), F32),
            vmem((768, 256), BF16),
            vmem((768, 256), BF16),
            vmem((2, 2, 256, 256), BF16),
            vmem((6, 256, 256), BF16),
            vmem((768, 2304), BF16),
            vmem((4, 256, 512), BF16),
            vmem((2, 768, 256), BF16),
            vmem((4, 512, 256), F32),
            vmem((3, 2, 256, 128), F32),
            vmem((8, 256), F32),
            vmem((2, 28, 256, 128), BF16),
            vmem((CHUNKS * TAPS, 256, 128), BF16),
            vmem((CHUNKS, TAPS, NY, NX, 16, 128), BF16),
            vmem((CHUNKS, 2, 4, 16, 128), BF16),
            vmem((CHUNKS, 2, 4, 16, 128), BF16),
            vmem((CHUNKS, TAPS, 4, 16, 128), BF16),
            vmem((CHUNKS, TAPS, 4, 16, 128), BF16),
            vmem((CHUNKS, TAPS, 4, 16, 128), F32),
            vmem((CHUNKS, 2, 16, 128), F32),
            vmem((CHUNKS, 2, 16, 128), F32),
            vmem((CHUNKS, TAPS, 16, 128), F32),
            vmem((CHUNKS, TAPS, 16, 128), F32),
            vmem((NZ, TAPS, 16, 128), F32),
            vmem((NZ, TAPS, 16, 128), F32),
            vmem((NZ, TAPS, 16, 128), BF16),
            vmem((NX, NZ, TAPS, 16, 128), BF16),
            vmem((NZ, 2 * NX, 8, 256), BF16),
            vmem((NZ, 2 * NX, 8, 256), BF16),
            vmem((NZ, 2 * NX, 8, 256), BF16),
            dma((1,)),
            dma((2, NZ)),
            dma((2, 2 * NX)),
            dma((2, 6)),
            dma((2, CHUNKS)),
            dma((2, CHUNKS, 4)),
            dma((2, CHUNKS, 4)),
            dma((2, NZ)),
            dma((2, NZ)),
            dma((2, 4, NZ)),
            dma((2, 4, NZ)),
            dma((2, 2, NZ)),
        ],
        compiler_params=pltpu.CompilerParams(collective_id=1, has_side_effects=True),
        cost_estimate=pl.CostEstimate(flops=5_500_000_000, bytes_accessed=12_000_000, transcendentals=2_000_000),
    )(latent_grad, frames, gain, weight, bias)


def finish_kernel(total, weight_grad, small):
    for core in range(2):
        lanes = pl.ds(core * 128, 128)
        for x in range(NX):
            rows = pl.ds(x * 16, 16)
            for tap in range(27):
                weight_grad[tap, rows, lanes] = total[core, x, tap // TAPS, tap % TAPS].astype(F32)
        sums = total[core, 0, 6, 3].astype(F32)
        row = sums[0:8] + pltpu.roll(sums[0:8], 6, 0)
        for side in range(2):

            @pl.when(lax.axis_index("tm") == 2 * core + side)
            def _():
                small[...] = row[:, 64 * side : 64 * side + 64]


def finish(total):
    return pl.pallas_call(
        finish_kernel,
        out_shape=(jax.ShapeDtypeStruct((27, 64, 256), F32), jax.ShapeDtypeStruct((8, 64), F32)),
        in_specs=[pl.BlockSpec(memory_space=pltpu.VMEM)],
        out_specs=[pl.BlockSpec(memory_space=pltpu.VMEM)] * 2,
    )(total)


def on_device(frames, norm_gain, conv_weight, conv_bias, latent_grad):
    frames_grad, latent, total = whole(
        latent_grad.reshape(4, 128, 256), frames, norm_gain.reshape(1, 256),
        conv_weight.reshape(3, 9, 256, 256), conv_bias.reshape(1, 256),
    )
    weight_grad, small = finish(total)
    return (
        latent.reshape(4, 64, 2, 256), frames_grad, weight_grad.reshape(3, 3, 3, 64, 256), small[0], small[1],
    )


def solution(mesh):
    placed = (P("tm", "rows", None, None), P(), P(), P(), P("tm", None, "rows", None))
    return jax.shard_map(
        on_device,
        mesh=mesh,
        in_specs=placed,
        out_specs=(
            P("tm", None, "rows", None),
            P("tm", "rows", None, None),
            P(None, None, None, "tm", None),
            P("tm"),
            P("tm"),
        ),
        check_vma=False,
    )
```

time: 128 us -> 99 us (0.77)
  starting transfers between devices: 23.6 us -> 0 us
  waiting for transfers between devices: 18.4 us -> 0 us
  Pallas kernels: 73.2 us -> 91 us
  local copies, waits for them, and re-layouts: 11.6 us -> 7.05 us
    pallas_call x2 -> x1, Pallas kernels: 70.7 us -> 88.5 us  [whole(): pl.pallas_call(whole_kernel, out_shape=(jax.ShapeDtypeStruct((4, 2, 256,...]
    all_to_all x1 -> x0, starting transfers between devices: 12.4 us -> none  [on_device(): lax.all_to_all(latent_grad, 'rows', split_axis=1, concat_axis=2, tiled=True)]
    ppermute x4 -> x0, starting transfers between devices: 11.1 us -> none  [shifted(): lax.ppermute(value, axis, [(source, source + steps) for source in range(l...]
    all_to_all x1 -> x0, waiting for transfers between devices: 9.5 us -> none  [on_device(): lax.all_to_all(latent_grad, 'rows', split_axis=1, concat_axis=2, tiled=True)]
    ppermute x4 -> x0, waiting for transfers between devices: 8.92 us -> none  [shifted(): lax.ppermute(value, axis, [(source, source + steps) for source in range(l...]
    slice x4 -> x0, local copies, waits for them, and re-layouts: 1.32 us -> none  [the longest x1 1.08 us: on_device(): early = shifted(frames[2:], 'tm', 1)]
    reshape x6 -> x2, local copies, waits for them, and re-layouts: 4.07 us -> 3.51 us  [the longest x1 1.75 us: on_device(): latent_grad.reshape(4, 128, 256)]
    unnamed x7 -> x1, local copies, waits for them, and re-layouts: 2.77 us -> 2.26 us
  transfers between devices with their start and end apart: 5 -> 0, of which waited for: 3 -> 0; matrix products, arithmetic and copies ran while one was open for 3% -> 0% of each run, Pallas kernels for 0% -> 0%
where the time goes in v3:
time: 99 us; the launch traced here: 98.7 us
  Pallas kernels  91 us (92%)
  local copies, waits for them, and re-layouts  7.05 us (7%)
    pallas_call x1, Pallas kernels, whole(): pl.pallas_call(whole_kernel, out_shape=(jax.ShapeDtypeStruct((4, 2, 256,...  88.5 us
    pallas_call x1, Pallas kernels, finish(): pl.pallas_call(finish_kernel, out_shape=(jax.ShapeDtypeStruct((27, 64, 25...  2.52 us
    unnamed x1, local copies, waits for them, and re-layouts  2.26 us

profile of v3, /device:TPU:1, one launch (start us, length us, event | category | flops | bytes accessed | tf_op | source)
XLA Modules:
  0.0 98.7 jit_solution(11502160206514350509)
XLA Ops:
  0.6 1.8 %reshape.28.latent_grad = bf16[4,128,256]{2,1,0:T(8,128)(2,1)} reshape(bf16[4,64,2,256]{3,2,1,0:T(2,128)(2,1)} %param.9) | data formatting | bytes 524288 | tf_op jit(solution)/shard_map/reshape | solution.py:621
  2.4 88.5 %shard_map.92 = (bf16[4,2,256,256]{3,2,1,0:T(8,128)(2,1)}, bf16[4,128,256]{2,1,0:T(8,128)(2,1)}, bf16[2,4,7,4,16,128]{5,4,3,2,1,0:T(8,128)(2,1)}) custom-call(bf16[4,128,256]{2,1,0:T(8,128)(2,1)} %reshape.28.latent_grad, bf16[4,2,256,256]{3,2,1,0:T(8,128)(2,1)} %frames.1, f32[1,256]{1,0:T(1,128)} %bitcast.10, bf16[3,9,256,256]{3,2,1,0:T(8,128)(2,1)} %bitcast.8, ...), custom_call_target="tpu_custom_call" | custom-call | flops 5500000256 | bytes 12000000 | tf_op jit(solution)/shard_map/pallas_call | solution.py:531
  90.9 1.8 %reshape.32 = bf16[4,64,2,256]{3,2,1,0:T(2,128)(2,1)} reshape(bf16[4,128,256]{2,1,0:T(8,128)(2,1)} %get-tuple-element.10) | data formatting | bytes 524288 | tf_op jit(solution)/shard_map/reshape | solution.py:626
  92.7 2.5 %shard_map.93 = (f32[27,64,256]{2,1,0:T(8,128)}, f32[8,64]{1,0:T(8,128)}) custom-call(bf16[2,4,7,4,16,128]{5,4,3,2,1,0:T(8,128)(2,1)} %get-tuple-element.12.total), custom_call_target="tpu_custom_call" | custom-call | tf_op jit(solution)/shard_map/pallas_call | solution.py:611
  95.2 1.3 %slice_bitcast_fusion = (f32[64]{0:T(128)}, f32[64]{0:T(128)}) fusion(f32[8,64]{1,0:T(8,128)} %get-tuple-element.14), kind=kLoop, calls=%fused_computation | loop fusion | bytes 1024 | tf_op jit(solution)/shard_map/squeeze | solution.py:626
  96.4 2.3 %copy.11 = bf16[4,2,256,256]{3,2,1,0:T(8,128)(2,1)} copy(bf16[4,2,256,256]{3,2,1,0:T(8,128)(2,1)} %get-tuple-element.23) | data formatting | bytes 2097152

commit v4 on v3

--- a/solution.py
+++ b/solution.py
@@ -34,7 +34,7 @@
     mid, first_plus2, first_minus2, second_plus2, second_minus2,
     low, arrive, total, block, latent_in, latent_mid, latent_out,
     weight_sem, gz_sem, gs_sem, near_sem,
-    core_sem, ring_sem, ring2_sem, z_sem, zback_sem, x_sem, pair_sem, lat_sem,
+    core_sem, ring_sem, ring2_sem, z_sem, zback_sem, x_sem, pair_sem, lz_sem, ls_sem,
 ):
     rows_at = lax.axis_index("rows")
     y = lax.axis_index("tm")
@@ -86,7 +86,7 @@
 
     for frame in range(4):
         for half in range(2):
-            woven[frame, half] = latent_grad[frame, :, pl.ds(half * 128, 128)].astype(F32)
+            woven[frame, half] = latent_grad[frame, :, :, pl.ds(half * 128, 128)].reshape(128, 128).astype(F32)
     unweave(blocks)
 
     pl.semaphore_wait(barrier, len(friends))
@@ -118,12 +118,25 @@
             for action in actions:
                 action()
 
-    g_outer = [
-        send(blocks.at[(z + step) % NZ], middle.at[z], gz_sem, (step,), along("z", step)) for step in range(1, NZ)
-    ]
+    order = (0, 1, 7, 2, 6, 3, 5, 4)
+
+    def hop_one(source, between, sems):
+        return [
+            send(source.at[(z + step) % NZ], between.at[z], sems, (step,), along("z", step)) for step in order[1:]
+        ]
+
+    def hop_two(between, target, sems, step):
+        at = (z - step + NZ) % NZ
+        return [
+            send(between.at[at, (slab + move) % (2 * NX)], target.at[at, slab], sems, (step, move), along("slab", move))
+            for move in range(1, 2 * NX)
+        ]
+
+    g_outer = hop_one(blocks, middle, gz_sem)
     only(has_future, early_on.start)
     only(has_above, below_own.start)
     middle[z] = blocks[z]
+    g_inner = hop_two(middle, landed, gs_sem, 0)
 
     @pl.when(jnp.logical_not(has_past))
     def _():
@@ -169,12 +182,9 @@
         hidden_tile(frames.at[at - 2, 0], at, 0, True)
         hidden_tile(frames.at[at - 2, 1], at, 1, True)
 
-    for copy in g_outer:
+    for copy, step in zip(g_outer, order[1:]):
         copy.wait_recv()
-    g_inner = [
-        send(middle.at[:, (slab + step) % (2 * NX)], landed.at[:, slab], gs_sem, (step,), along("slab", step))
-        for step in range(1, 2 * NX)
-    ]
+        g_inner += hop_two(middle, landed, gs_sem, step)
     landed[:, slab] = middle[:, slab]
     spread[...] = jnp.zeros_like(spread)
     gain_sum[...] = jnp.zeros_like(gain_sum)
@@ -259,14 +269,19 @@
         sent[0].wait_recv()
         sent[1].wait_recv()
         own = piece(source, chunk, stage, here(axis, 0), ALL)[...].astype(F32)
-        (mid, low)[stage][chunk] = own + plus_in[chunk].astype(F32) + minus_in[chunk].astype(F32)
-
-    def to_owner(chunk):
-        step = (chunk - z + NZ) % NZ
-        return pltpu.make_async_remote_copy(
-            src_ref=low.at[chunk], dst_ref=arrive.at[step], send_sem=z_sem.at[0, chunk], recv_sem=z_sem.at[1, step],
-            device_id=(row_of(chunk, x, core), y), device_id_type=MESH,
-        )
+        summed = own + plus_in[chunk].astype(F32) + minus_in[chunk].astype(F32)
+        if stage == 0:
+            mid[chunk] = summed
+        else:
+            low[chunk] = summed.reshape(NZ, 8, 128)
+
+    shares = {}
+
+    def to_owners(chunk):
+        shares[chunk] = [
+            send(low.at[chunk, (z + step) % NZ], arrive.at[step, chunk], z_sem, (chunk, step), along("z", step))
+            for step in order[1:]
+        ]
 
     opened, sent, opened2, sent2 = {}, {}, {}, {}
 
@@ -293,17 +308,25 @@
     def close_two(*chunks):
         for chunk in chunks:
             ring_close(chunk, 1, sent2[chunk])
-            only(z != chunk, to_owner(chunk).start)
+            to_owners(chunk)
 
     step_on(0, grad, range(4))
     weight_taps(5)
     pair_send(5)
+    only(has_past, early_on.wait_recv)
+    only(has_above, below_early.start)
+
+    @pl.loop(0, 2)
+    def _(at):
+        hidden_tile(early.at[at, 0], at, 0, False)
+        hidden_tile(early.at[at, 1], at, 1, False)
+
+    pair_close(5)
     only(has_future, grad_late.wait_recv)
     only(has_below, above_late.start)
     step_on(0, grad, (4, 5))
     weight_taps(0)
     pair_send(0)
-    pair_close(5)
     only(has_above, above_own.wait_recv, above_late.wait_recv)
     step_on(1, grad_above, range(6))
     before = 0
@@ -312,8 +335,6 @@
         pair_send(chunk)
         pair_close(before)
         before = chunk
-    only(has_past, early_on.wait_recv)
-    only(has_above, below_early.start)
 
     def back_taps(tap):
         where = pl.ds((2 - tap) * 128, 512)
@@ -350,13 +371,11 @@
 
     back_taps(0)
     pair_close(before)
+    back_taps(1)
+    back_taps(2)
     next_one(5, 0)
-    back_taps(1)
+    frame_back(0, 2)
     next_one(3, 1)
-    back_taps(2)
-    next_one(2, 4)
-    frame_back(0, 2)
-    close_one(5, 0)
     frame_back(2, 4)
 
     gain_local = jnp.sum(gain_sum[...], axis=0, keepdims=True)
@@ -370,24 +389,15 @@
     parts[1, 27] = small[:, 128:]
     weight_taps(6)
     pair_send(6)
-    close_one(3, 1)
-
-    @pl.loop(0, 2)
-    def _(at):
-        hidden_tile(early.at[at, 0], at, 0, False)
-        hidden_tile(early.at[at, 1], at, 1, False)
-
-    pair_close(6)
-    close_one(2, 4)
-    next_two(5, 0)
+    next_one(2, 4)
     only(has_below, below_own.wait_recv, below_early.wait_recv)
 
     @pl.loop(0, 6)
     def _(at):
         hidden_tile(below.at[at], at, 2, False)
 
-    next_one(6)
-    next_two(3, 1)
+    pair_close(6)
+    close_one(5, 0)
     spread[0] = jnp.broadcast_to(bias[...], (512, 256))
 
     @pl.loop(0, 3)
@@ -395,43 +405,47 @@
         where = pl.ds(pl.multiple_of(tap * 128, 128), 512)
         spread[0] += dot_nn(columns[where, :], weight[tap].reshape(2304, 256))
 
-    next_two(2, 4)
-    close_one(6)
-    close_two(5, 0, 3, 1)
     for frame in range(4):
         for half in range(2):
             woven[frame, half] = spread[0, pl.ds(frame * 128, 128), pl.ds(half * 128, 128)]
     unweave(latent_in)
-    outer = [
-        send(latent_in.at[(z + step) % NZ], latent_mid.at[z], lat_sem, (0, step), along("z", step))
-        for step in range(1, NZ)
-    ]
+    outer = hop_one(latent_in, latent_mid, lz_sem)
     latent_mid[z] = latent_in[z]
+    close_one(3, 1)
+    next_one(6)
+    close_one(2, 4)
+    next_two(5, 0, 3, 1)
+    close_one(6)
+    inner = hop_two(latent_mid, latent_out, ls_sem, 0)
+    next_two(2, 4)
+    close_two(5, 0, 3, 1)
     next_two(6)
-    close_two(2, 4, 6)
-    started = list(pair.values()) + outer + g_outer + g_inner
-    for table in (opened, sent, opened2, sent2):
+    close_two(2, 4)
+    for copy, step in zip(outer, order[1:]):
+        copy.wait_recv()
+        inner += hop_two(latent_mid, latent_out, ls_sem, step)
+    latent_out[:, slab] = latent_mid[:, slab]
+    close_two(6)
+    started = list(pair.values()) + outer + inner + g_outer + g_inner
+    for table in (opened, sent, opened2, sent2, shares):
         for chunk in range(CHUNKS):
             started += table[chunk]
 
+    for chunk in (5, 0, 3, 1, 2, 4, 6):
+        summed = low[chunk, z]
+        for copy, step in zip(shares[chunk], order[1:]):
+            copy.wait_recv()
+            summed += arrive[step, chunk]
+        total[z, chunk] = summed.astype(BF16)
+
     def back(step):
         return copy_to(total.at[z], total.at[z], zback_sem, (step,), along("z", step))
 
-    @pl.when(z < CHUNKS)
-    def _():
-        summed = low[z]
-        for step in range(1, NZ):
-            pltpu.make_async_remote_copy(
-                src_ref=low.at[0], dst_ref=arrive.at[step], send_sem=z_sem.at[0, 0], recv_sem=z_sem.at[1, step],
-                device_id=sibling, device_id_type=MESH,
-            ).wait_recv()
-            summed += arrive[step]
-        total[z] = summed.astype(BF16)
-        for step in range(1, NZ):
-            back(step).start()
+    for step in order[1:]:
+        back(step).start()
 
     right, left, across = (x + 1) % NX, (x + 3) % NX, (x + 2) % NX
-    order = (0, 1, 7, 2, 6, 3, 5, 4)
+    HALF, REST = pl.ds(0, 4), pl.ds(4, 3)
 
     def to_right(step, at):
         return copy_to(total.at[at], block.at[x, at], x_sem, (0, step), along("x", 1))
@@ -440,11 +454,11 @@
         return copy_to(total.at[at], block.at[x, at], x_sem, (1, step), along("x", 3))
 
     def on_right(step, at):
-        half = block.at[left, at, FIRST]
+        half = block.at[left, at, HALF]
         return copy_to(half, half, x_sem, (2, step), along("x", 1))
 
     def on_left(step, at):
-        half = block.at[right, at, LAST]
+        half = block.at[right, at, REST]
         return copy_to(half, half, x_sem, (3, step), along("x", 3))
 
     def across_core(which, step, at):
@@ -454,11 +468,7 @@
 
     def each(body):
         for step in order:
-            at = (z - step + NZ) % NZ
-
-            @pl.when(at < CHUNKS)
-            def _():
-                body(step, at)
+            body(step, (z - step + NZ) % NZ)
 
     def fan_one(step, at):
         if step:
@@ -492,15 +502,7 @@
         on_right(step, at).wait_send()
         on_left(step, at).wait_send()
 
-    for copy in outer:
-        copy.wait_recv()
-    inner = [
-        send(latent_mid.at[:, (slab + step) % (2 * NX)], latent_out.at[:, slab], lat_sem, (1, step), along("slab", step))
-        for step in range(1, 2 * NX)
-    ]
-    latent_out[:, slab] = latent_mid[:, slab]
     each(fan_one)
-    each(fan_two)
     for copy in inner:
         copy.wait_recv()
 
@@ -508,21 +510,17 @@
         latent[frame, :, pl.ds(half * 128, 128)] = value
 
     weave(latent_out, put_latent)
+    each(fan_two)
     each(fan_three)
-    for copy in started + inner:
+    for copy in started:
         copy.wait_send()
     each(fan_last)
     only(has_future, early_on.wait_send)
     only(has_above, below_own.wait_send, below_early.wait_send)
     only(has_past, grad_late.wait_send)
     only(has_below, above_own.wait_send, above_late.wait_send)
-    for chunk in range(CHUNKS):
-        only(z != chunk, to_owner(chunk).wait_send)
-
-    @pl.when(z < CHUNKS)
-    def _():
-        for step in range(1, NZ):
-            back(step).wait_send()
+    for step in order[1:]:
+        back(step).wait_send()
 
 
 def whole(latent_grad, frames, gain, weight, bias):
@@ -533,7 +531,7 @@
         out_shape=(
             jax.ShapeDtypeStruct((4, 2, 256, 256), BF16),
             jax.ShapeDtypeStruct((4, 128, 256), BF16),
-            jax.ShapeDtypeStruct((2, NX, CHUNKS, TAPS, 16, 128), BF16),
+            jax.ShapeDtypeStruct((2, NX, NZ, CHUNKS, 8, 128), BF16),
         ),
         in_specs=[inside, inside, inside, pl.BlockSpec(memory_space=pl.ANY), inside],
         out_specs=[inside] * 3,
@@ -566,64 +564,110 @@
             vmem((CHUNKS, 2, 16, 128), F32),
             vmem((CHUNKS, TAPS, 16, 128), F32),
             vmem((CHUNKS, TAPS, 16, 128), F32),
-            vmem((NZ, TAPS, 16, 128), F32),
-            vmem((NZ, TAPS, 16, 128), F32),
-            vmem((NZ, TAPS, 16, 128), BF16),
-            vmem((NX, NZ, TAPS, 16, 128), BF16),
+            vmem((CHUNKS, NZ, 8, 128), F32),
+            vmem((NZ, CHUNKS, 8, 128), F32),
+            vmem((NZ, CHUNKS, 8, 128), BF16),
+            vmem((NX, NZ, CHUNKS, 8, 128), BF16),
             vmem((NZ, 2 * NX, 8, 256), BF16),
             vmem((NZ, 2 * NX, 8, 256), BF16),
             vmem((NZ, 2 * NX, 8, 256), BF16),
             dma((1,)),
             dma((2, NZ)),
-            dma((2, 2 * NX)),
+            dma((2, NZ, 2 * NX)),
             dma((2, 6)),
             dma((2, CHUNKS)),
             dma((2, CHUNKS, 4)),
             dma((2, CHUNKS, 4)),
-            dma((2, NZ)),
+            dma((2, CHUNKS, NZ)),
             dma((2, NZ)),
             dma((2, 4, NZ)),
             dma((2, 4, NZ)),
-            dma((2, 2, NZ)),
+            dma((2, NZ)),
+            dma((2, NZ, 2 * NX)),
         ],
         compiler_params=pltpu.CompilerParams(collective_id=1, has_side_effects=True),
         cost_estimate=pl.CostEstimate(flops=5_500_000_000, bytes_accessed=12_000_000, transcendentals=2_000_000),
     )(latent_grad, frames, gain, weight, bias)
 
 
-def finish_kernel(total, weight_grad, small):
+def finish_kernel(
+    total_far, frames_far, latent_far, weight_grad, frames_grad, latent, gain_grad, bias_grad,
+    total, frames_near, latent_near, latent_wide, wide, sems,
+):
+    copy = pltpu.make_async_copy
+    total_in = copy(total_far, total, sems.at[0])
+    frames_in = copy(frames_far, frames_near, sems.at[1])
+    latent_in = copy(latent_far, latent_near, sems.at[2])
+    total_in.start()
+    frames_in.start()
+    latent_in.start()
+    total_in.wait()
+    going = []
+    for chunk in range(CHUNKS):
+        for tap in range(chunk * TAPS, min(27, chunk * TAPS + TAPS)):
+            for core in range(2):
+                for x in range(NX):
+                    for side in range(2):
+                        part = total[core, x, 2 * (tap % TAPS) + side, chunk]
+                        wide[tap, pl.ds(x * 16 + side * 8, 8), pl.ds(core * 128, 128)] = part.astype(F32)
+        taps = pl.ds(chunk * TAPS, min(27, chunk * TAPS + TAPS) - chunk * TAPS)
+        going.append(copy(wide.at[taps], weight_grad.at[taps], sems.at[3 + chunk]))
+        going[-1].start()
+        if chunk == 1:
+            frames_in.wait()
+            going.append(copy(frames_near, frames_grad, sems.at[10]))
+            going[-1].start()
+        if chunk == 3:
+            latent_in.wait()
+            for frame in range(4):
+                latent_wide[frame] = latent_near[frame].reshape(64, 2, 256)
+            going.append(copy(latent_wide, latent, sems.at[11]))
+            going[-1].start()
     for core in range(2):
-        lanes = pl.ds(core * 128, 128)
-        for x in range(NX):
-            rows = pl.ds(x * 16, 16)
-            for tap in range(27):
-                weight_grad[tap, rows, lanes] = total[core, x, tap // TAPS, tap % TAPS].astype(F32)
-        sums = total[core, 0, 6, 3].astype(F32)
-        row = sums[0:8] + pltpu.roll(sums[0:8], 6, 0)
+        sums = total[core, 0, 6, 6].astype(F32)
+        row = sums + pltpu.roll(sums, 6, 0)
         for side in range(2):
 
             @pl.when(lax.axis_index("tm") == 2 * core + side)
             def _():
-                small[...] = row[:, 64 * side : 64 * side + 64]
-
-
-def finish(total):
+                gain_grad[...] = row[0:1, 64 * side : 64 * side + 64]
+                bias_grad[...] = row[1:2, 64 * side : 64 * side + 64]
+
+    for item in going:
+        item.wait()
+
+
+def finish(total, frames_grad, latent):
+    inside, far = pl.BlockSpec(memory_space=pltpu.VMEM), pl.BlockSpec(memory_space=pl.ANY)
     return pl.pallas_call(
         finish_kernel,
-        out_shape=(jax.ShapeDtypeStruct((27, 64, 256), F32), jax.ShapeDtypeStruct((8, 64), F32)),
-        in_specs=[pl.BlockSpec(memory_space=pltpu.VMEM)],
-        out_specs=[pl.BlockSpec(memory_space=pltpu.VMEM)] * 2,
-    )(total)
+        out_shape=(
+            jax.ShapeDtypeStruct((27, 64, 256), F32),
+            jax.ShapeDtypeStruct((4, 2, 256, 256), BF16),
+            jax.ShapeDtypeStruct((4, 64, 2, 256), BF16),
+            jax.ShapeDtypeStruct((1, 64), F32),
+            jax.ShapeDtypeStruct((1, 64), F32),
+        ),
+        in_specs=[far] * 3,
+        out_specs=[far, far, far, inside, inside],
+        scratch_shapes=[
+            pltpu.VMEM((2, NX, NZ, CHUNKS, 8, 128), BF16),
+            pltpu.VMEM((4, 2, 256, 256), BF16),
+            pltpu.VMEM((4, 128, 256), BF16),
+            pltpu.VMEM((4, 64, 2, 256), BF16),
+            pltpu.VMEM((27, 64, 256), F32),
+            pltpu.SemaphoreType.DMA((12,)),
+        ],
+    )(total, frames_grad, latent)
 
 
 def on_device(frames, norm_gain, conv_weight, conv_bias, latent_grad):
     frames_grad, latent, total = whole(
-        latent_grad.reshape(4, 128, 256), frames, norm_gain.reshape(1, 256),
-        conv_weight.reshape(3, 9, 256, 256), conv_bias.reshape(1, 256),
+        latent_grad, frames, norm_gain.reshape(1, 256), conv_weight.reshape(3, 9, 256, 256), conv_bias.reshape(1, 256),
     )
-    weight_grad, small = finish(total)
+    weight_grad, frames_grad, latent, gain_grad, bias_grad = finish(total, frames_grad, latent)
     return (
-        latent.reshape(4, 64, 2, 256), frames_grad, weight_grad.reshape(3, 3, 3, 64, 256), small[0], small[1],
+        latent, frames_grad, weight_grad.reshape(3, 3, 3, 64, 256), gain_grad.reshape(64), bias_grad.reshape(64),
     )
 
 

time: 99 us -> 88.2 us (0.89)
  local copies, waits for them, and re-layouts: 7.05 us -> 0 us
  Pallas kernels: 91 us -> 87.5 us
    pallas_call x1, Pallas kernels: 88.5 us -> 83.9 us  [whole(): pl.pallas_call(whole_kernel, out_shape=(jax.ShapeDtypeStruct((4, 2, 256,...]
    reshape x2 -> x0, local copies, waits for them, and re-layouts: 3.51 us -> none  [the longest x1 1.75 us: on_device(): latent_grad.reshape(4, 128, 256)]
    unnamed x1 -> x0, local copies, waits for them, and re-layouts: 2.26 us -> none
    squeeze x1 -> x0, local copies, waits for them, and re-layouts: 1.28 us -> none  [on_device(): small[1]]
    pallas_call x1, Pallas kernels: 2.52 us -> 3.57 us  [finish(): pl.pallas_call(finish_kernel, out_shape=(jax.ShapeDtypeStruct((27, 64, 25...]
where the time goes in v4:
time: 88.2 us; the launch traced here: 88.1 us
  Pallas kernels  87.5 us (99%)
    pallas_call x1, Pallas kernels, whole(): pl.pallas_call(whole_kernel, out_shape=(jax.ShapeDtypeStruct((4, 2, 256,...  83.9 us
    pallas_call x1, Pallas kernels, finish(): pl.pallas_call(finish_kernel, out_shape=(jax.ShapeDtypeStruct((27, 64, 25...  3.57 us

profile of v4, /device:TPU:1, one launch (start us, length us, event | category | flops | bytes accessed | tf_op | source)
XLA Modules:
  0.0 88.1 jit_solution(8509892591173544690)
XLA Ops:
  0.6 83.9 %shard_map.92 = (bf16[4,2,256,256]{3,2,1,0:T(8,128)(2,1)}, bf16[4,128,256]{2,1,0:T(8,128)(2,1)}, bf16[2,4,8,7,8,128]{5,4,3,2,1,0:T(8,128)(2,1)}) custom-call(bf16[4,64,2,256]{3,2,1,0:T(2,128)(2,1)} %latent_grad.1, bf16[4,2,256,256]{3,2,1,0:T(8,128)(2,1)} %frames.1, f32[1,256]{1,0:T(1,128)} %bitcast.8, bf16[3,9,256,256]{3,2,1,0:T(8,128)(2,1)} %bitcast.6, ...), custom_call_target="tpu_custom_call" | custom-call | flops 5500000256 | bytes 12000000 | tf_op jit(solution)/shard_map/pallas_call | solution.py:529
  84.5 3.6 %shard_map.93 = (f32[27,64,256]{2,1,0:T(8,128)}, bf16[4,2,256,256]{3,2,1,0:T(8,128)(2,1)}, bf16[4,64,2,256]{3,2,1,0:T(2,128)(2,1)}, f32[1,64]{1,0:T(1,128)}, f32[1,64]{1,0:T(1,128)}) custom-call(bf16[2,4,8,7,8,128]{5,4,3,2,1,0:T(8,128)(2,1)} %get-tuple-element.13.total_far, bf16[4,2,256,256]{3,2,1,0:T(8,128)(2,1)} %get-tuple-element.14.frames_far, ...), custom_call_target="tpu_custom_call" | custom-call | tf_op jit(solution)/shard_map/pallas_call | solution.py:642

commit v5 on v4

--- a/solution.py
+++ b/solution.py
@@ -26,15 +26,16 @@
 
 
 def whole_kernel(
-    latent_grad, frames, gain, weight_far, bias,
-    frames_grad, latent, result,
+    latent_grad_far, frames_far, gain, weight_far, bias,
+    frames_grad_far, latent_far, result, note_out,
+    latent_grad, frames, frames_grad, latent, sib, note, note_pair, note_y, note_x, note_z, note_end,
     weight, blocks, middle, landed, flat, woven, grad, grad_above, early, below,
     columns, turned, grad_next, spread, tile, gain_sum, parts,
     other, mine, first_plus, first_minus, second_plus, second_minus,
     mid, first_plus2, first_minus2, second_plus2, second_minus2,
     low, arrive, total, block, latent_in, latent_mid, latent_out,
     weight_sem, gz_sem, gs_sem, near_sem,
-    core_sem, ring_sem, ring2_sem, z_sem, zback_sem, x_sem, pair_sem, lz_sem, ls_sem,
+    core_sem, ring_sem, ring2_sem, z_sem, zback_sem, x_sem, pair_sem, lz_sem, ls_sem, note_sem, out_sem,
 ):
     rows_at = lax.axis_index("rows")
     y = lax.axis_index("tm")
@@ -58,14 +59,18 @@
             return ((rows_at + step + count) % count, y)
         return (row_of((z + step) % NZ, x, core), y)
 
-    weight_in = pltpu.make_async_copy(weight_far, weight, weight_sem.at[0])
-    weight_in.start()
-
     barrier = pltpu.get_barrier_semaphore()
     friends = [along("z", step) for step in range(1, NZ)] + [along("slab", step) for step in range(1, 2 * NX)]
-    friends += [along("y", 1), along("y", -1), along("row", 1), along("row", -1)]
+    friends += [along("y", 1), along("y", 2), along("y", -1), along("row", 1), along("row", -1)]
     for friend in friends:
         pl.semaphore_signal(barrier, inc=1, device_id=friend, device_id_type=MESH)
+    latent_grad_in = pltpu.make_async_copy(latent_grad_far, latent_grad, weight_sem.at[1])
+    frames_in = pltpu.make_async_copy(frames_far, frames, weight_sem.at[2])
+    weight_in = pltpu.make_async_copy(weight_far, weight, weight_sem.at[0])
+    latent_grad_in.start()
+    frames_in.start()
+    weight_in.start()
+    latent_grad_in.wait()
 
     def unweave(target):
         for frame in range(4):
@@ -133,6 +138,7 @@
         ]
 
     g_outer = hop_one(blocks, middle, gz_sem)
+    frames_in.wait()
     only(has_future, early_on.start)
     only(has_above, below_own.start)
     middle[z] = blocks[z]
@@ -330,7 +336,8 @@
     only(has_above, above_own.wait_recv, above_late.wait_recv)
     step_on(1, grad_above, range(6))
     before = 0
-    for chunk in (3, 1, 2, 4):
+    parts[:, 27] = jnp.zeros((2, 256, 128), BF16)
+    for chunk in (3, 1, 2, 4, 6):
         weight_taps(chunk)
         pair_send(chunk)
         pair_close(before)
@@ -369,35 +376,51 @@
                     mean = jnp.mean(unit_grad * unit, axis=-1, keepdims=True)
                     frames_grad[at, row, rows, :] = (inv * (unit_grad - unit * mean)).astype(BF16)
 
+    def spread_out(source, bank, me, axis, total_at, stage):
+        bank[me] = source
+        return [
+            send(bank.at[me], bank.at[me], note_sem, (stage, step), along(axis, step)) for step in range(1, total_at)
+        ]
+
+    def collect(copies, bank, total_at):
+        for copy in copies:
+            copy.wait_recv()
+        value = bank[0]
+        for at in range(1, total_at):
+            value = value + bank[at]
+        return value
+
     back_taps(0)
     pair_close(before)
     back_taps(1)
+    next_one(5, 0)
     back_taps(2)
-    next_one(5, 0)
+    next_one(3, 1)
     frame_back(0, 2)
-    next_one(3, 1)
+    next_one(2, 4)
     frame_back(2, 4)
-
+    frames_out = pltpu.make_async_copy(frames_grad, frames_grad_far, out_sem.at[0])
+    frames_out.start()
     gain_local = jnp.sum(gain_sum[...], axis=0, keepdims=True)
     bias_local = jnp.sum(grad[pl.ds(0, 512), :].astype(F32), axis=0, keepdims=True)
-    gain_rest = gain_local - gain_local.astype(BF16).astype(F32)
-    bias_rest = bias_local - bias_local.astype(BF16).astype(F32)
-    spot = lax.broadcasted_iota(jnp.int32, (256, 256), 0) % 64
+    spot = lax.broadcasted_iota(jnp.int32, (8, 256), 0)
     small = jnp.where(spot == 0, gain_local, jnp.where(spot == 1, bias_local, 0.0))
-    small = jnp.where(spot == 2, gain_rest, jnp.where(spot == 3, bias_rest, small)).astype(BF16)
-    parts[0, 27] = small[:, :128]
-    parts[1, 27] = small[:, 128:]
-    weight_taps(6)
-    pair_send(6)
-    next_one(2, 4)
+    note[0] = small[:, :128]
+    note[1] = small[:, 128:]
+    notes = [send(note.at[1 - core], note_pair, note_sem, (0, 1), sibling)]
+    next_one(6)
+    close_one(5, 0, 3, 1)
+    notes[0].wait_recv()
+    notes_y = spread_out(note[core] + note_pair[...], note_y, y, "y", NY, 1)
     only(has_below, below_own.wait_recv, below_early.wait_recv)
 
     @pl.loop(0, 6)
     def _(at):
         hidden_tile(below.at[at], at, 2, False)
 
-    pair_close(6)
-    close_one(5, 0)
+    close_one(2, 4, 6)
+    next_two(5, 0, 3, 1)
+    notes_x = spread_out(collect(notes_y, note_y, NY), note_x, x, "x", NX, 2)
     spread[0] = jnp.broadcast_to(bias[...], (512, 256))
 
     @pl.loop(0, 3)
@@ -405,28 +428,18 @@
         where = pl.ds(pl.multiple_of(tap * 128, 128), 512)
         spread[0] += dot_nn(columns[where, :], weight[tap].reshape(2304, 256))
 
+    next_two(2, 4, 6)
+    close_two(5, 0, 3, 1)
     for frame in range(4):
         for half in range(2):
             woven[frame, half] = spread[0, pl.ds(frame * 128, 128), pl.ds(half * 128, 128)]
     unweave(latent_in)
+    close_two(2, 4, 6)
     outer = hop_one(latent_in, latent_mid, lz_sem)
     latent_mid[z] = latent_in[z]
-    close_one(3, 1)
-    next_one(6)
-    close_one(2, 4)
-    next_two(5, 0, 3, 1)
-    close_one(6)
     inner = hop_two(latent_mid, latent_out, ls_sem, 0)
-    next_two(2, 4)
-    close_two(5, 0, 3, 1)
-    next_two(6)
-    close_two(2, 4)
-    for copy, step in zip(outer, order[1:]):
-        copy.wait_recv()
-        inner += hop_two(latent_mid, latent_out, ls_sem, step)
-    latent_out[:, slab] = latent_mid[:, slab]
-    close_two(6)
-    started = list(pair.values()) + outer + inner + g_outer + g_inner
+    notes_z = spread_out(collect(notes_x, note_x, NX), note_z, z, "z", NZ, 3)
+    started = list(pair.values()) + g_outer + g_inner + notes + notes_y + notes_x + notes_z
     for table in (opened, sent, opened2, sent2, shares):
         for chunk in range(CHUNKS):
             started += table[chunk]
@@ -464,7 +477,7 @@
     def across_core(which, step, at):
         source = total.at[at] if which == 0 else block.at[(left, right, across)[which - 1], at]
         where = (x, left, right, across)[which]
-        return copy_to(source, result.at[core, where, at], pair_sem, (which, step), sibling)
+        return copy_to(source, sib.at[where, at], pair_sem, (which, step), sibling)
 
     def each(body):
         for step in order:
@@ -476,66 +489,98 @@
         to_right(step, at).start()
         to_left(step, at).start()
         across_core(0, step, at).start()
-        result[core, x, at] = total[at]
 
     def fan_two(step, at):
         to_right(step, at).wait_recv()
         on_right(step, at).start()
         across_core(1, step, at).start()
-        result[core, left, at] = block[left, at]
         to_left(step, at).wait_recv()
         on_left(step, at).start()
         across_core(2, step, at).start()
-        result[core, right, at] = block[right, at]
 
     def fan_three(step, at):
         on_right(step, at).wait_recv()
         on_left(step, at).wait_recv()
         across_core(3, step, at).start()
-        result[core, across, at] = block[across, at]
-
-    def fan_last(step, at):
+
+    def keep(source, half, where, at):
+        copy = pltpu.make_async_copy(source, result.at[half, where], out_sem.at[at])
+        copy.start()
+        return copy
+
+    each(fan_one)
+    kept = [frames_out, keep(total, core, x, 1)]
+    for copy, step in zip(outer, order[1:]):
+        copy.wait_recv()
+        inner += hop_two(latent_mid, latent_out, ls_sem, step)
+    latent_out[:, slab] = latent_mid[:, slab]
+    note_end[0] = collect(notes_z, note_z, NZ)
+    note_last = send(note_end.at[0], note_end.at[1], note_sem, (0, 2), sibling)
+    each(fan_two)
+    kept += [keep(block.at[left], core, left, 2), keep(block.at[right], core, right, 3)]
+    for copy in inner:
+        copy.wait_recv()
+
+    def put_latent(frame, half, value):
+        latent[frame, :, pl.ds(half * 128, 128)] = value
+
+    weave(latent_out, put_latent)
+    kept.append(pltpu.make_async_copy(latent, latent_far, out_sem.at[4]))
+    kept[-1].start()
+    each(fan_three)
+    kept.append(keep(block.at[across], core, across, 5))
+    note_last.wait()
+    note_out[core] = note_end[0]
+    note_out[1 - core] = note_end[1]
+    for which, where in enumerate((x, left, right, across)):
+        for step in order:
+            across_core(which, step, (z - step + NZ) % NZ).wait_recv()
+        kept.append(keep(sib.at[where], 1 - core, where, 6 + which))
+    for copy in started + outer + inner:
+        copy.wait_send()
+    for step in order:
+        at = (z - step + NZ) % NZ
         for which in range(4):
-            across_core(which, step, at).wait()
+            across_core(which, step, at).wait_send()
         to_right(step, at).wait_send()
         to_left(step, at).wait_send()
         on_right(step, at).wait_send()
         on_left(step, at).wait_send()
-
-    each(fan_one)
-    for copy in inner:
-        copy.wait_recv()
-
-    def put_latent(frame, half, value):
-        latent[frame, :, pl.ds(half * 128, 128)] = value
-
-    weave(latent_out, put_latent)
-    each(fan_two)
-    each(fan_three)
-    for copy in started:
-        copy.wait_send()
-    each(fan_last)
     only(has_future, early_on.wait_send)
     only(has_above, below_own.wait_send, below_early.wait_send)
     only(has_past, grad_late.wait_send)
     only(has_below, above_own.wait_send, above_late.wait_send)
     for step in order[1:]:
         back(step).wait_send()
+    for copy in kept:
+        copy.wait()
 
 
 def whole(latent_grad, frames, gain, weight, bias):
     dma, vmem = pltpu.SemaphoreType.DMA, pltpu.VMEM
-    inside = pl.BlockSpec(memory_space=pltpu.VMEM)
+    inside, far = pl.BlockSpec(memory_space=pltpu.VMEM), pl.BlockSpec(memory_space=pl.ANY)
     return pl.pallas_call(
         whole_kernel,
         out_shape=(
             jax.ShapeDtypeStruct((4, 2, 256, 256), BF16),
             jax.ShapeDtypeStruct((4, 128, 256), BF16),
             jax.ShapeDtypeStruct((2, NX, NZ, CHUNKS, 8, 128), BF16),
+            jax.ShapeDtypeStruct((2, 8, 128), F32),
         ),
-        in_specs=[inside, inside, inside, pl.BlockSpec(memory_space=pl.ANY), inside],
-        out_specs=[inside] * 3,
+        in_specs=[far, far, inside, far, inside],
+        out_specs=[far, far, far, inside],
         scratch_shapes=[
+            vmem((4, 64, 2, 256), BF16),
+            vmem((4, 2, 256, 256), BF16),
+            vmem((4, 2, 256, 256), BF16),
+            vmem((4, 128, 256), BF16),
+            vmem((NX, NZ, CHUNKS, 8, 128), BF16),
+            vmem((2, 8, 128), F32),
+            vmem((8, 128), F32),
+            vmem((NY, 8, 128), F32),
+            vmem((NX, 8, 128), F32),
+            vmem((NZ, 8, 128), F32),
+            vmem((2, 8, 128), F32),
             vmem((3, 9, 256, 256), BF16),
             vmem((NZ, 2 * NX, 8, 256), BF16),
             vmem((NZ, 2 * NX, 8, 256), BF16),
@@ -571,7 +616,7 @@
             vmem((NZ, 2 * NX, 8, 256), BF16),
             vmem((NZ, 2 * NX, 8, 256), BF16),
             vmem((NZ, 2 * NX, 8, 256), BF16),
-            dma((1,)),
+            dma((3,)),
             dma((2, NZ)),
             dma((2, NZ, 2 * NX)),
             dma((2, 6)),
@@ -584,6 +629,8 @@
             dma((2, 4, NZ)),
             dma((2, NZ)),
             dma((2, NZ, 2 * NX)),
+            dma((2, 4, NZ)),
+            dma((10,)),
         ],
         compiler_params=pltpu.CompilerParams(collective_id=1, has_side_effects=True),
         cost_estimate=pl.CostEstimate(flops=5_500_000_000, bytes_accessed=12_000_000, transcendentals=2_000_000),
@@ -591,19 +638,22 @@
 
 
 def finish_kernel(
-    total_far, frames_far, latent_far, weight_grad, frames_grad, latent, gain_grad, bias_grad,
+    total_far, frames_far, latent_far, note, weight_grad, frames_grad, latent, gain_grad, bias_grad,
     total, frames_near, latent_near, latent_wide, wide, sems,
 ):
     copy = pltpu.make_async_copy
-    total_in = copy(total_far, total, sems.at[0])
+    totals_in = [
+        copy(total_far.at[:, :, :, chunk], total.at[:, :, :, chunk], sems.at[12 + chunk]) for chunk in range(CHUNKS)
+    ]
     frames_in = copy(frames_far, frames_near, sems.at[1])
     latent_in = copy(latent_far, latent_near, sems.at[2])
-    total_in.start()
+    latent_in.start()
+    for item in totals_in:
+        item.start()
     frames_in.start()
-    latent_in.start()
-    total_in.wait()
     going = []
     for chunk in range(CHUNKS):
+        totals_in[chunk].wait()
         for tap in range(chunk * TAPS, min(27, chunk * TAPS + TAPS)):
             for core in range(2):
                 for x in range(NX):
@@ -613,7 +663,7 @@
         taps = pl.ds(chunk * TAPS, min(27, chunk * TAPS + TAPS) - chunk * TAPS)
         going.append(copy(wide.at[taps], weight_grad.at[taps], sems.at[3 + chunk]))
         going[-1].start()
-        if chunk == 1:
+        if chunk == 2:
             frames_in.wait()
             going.append(copy(frames_near, frames_grad, sems.at[10]))
             going[-1].start()
@@ -624,8 +674,7 @@
             going.append(copy(latent_wide, latent, sems.at[11]))
             going[-1].start()
     for core in range(2):
-        sums = total[core, 0, 6, 6].astype(F32)
-        row = sums + pltpu.roll(sums, 6, 0)
+        row = note[core]
         for side in range(2):
 
             @pl.when(lax.axis_index("tm") == 2 * core + side)
@@ -637,7 +686,7 @@
         item.wait()
 
 
-def finish(total, frames_grad, latent):
+def finish(total, frames_grad, latent, note):
     inside, far = pl.BlockSpec(memory_space=pltpu.VMEM), pl.BlockSpec(memory_space=pl.ANY)
     return pl.pallas_call(
         finish_kernel,
@@ -648,7 +697,7 @@
             jax.ShapeDtypeStruct((1, 64), F32),
             jax.ShapeDtypeStruct((1, 64), F32),
         ),
-        in_specs=[far] * 3,
+        in_specs=[far] * 3 + [inside],
         out_specs=[far, far, far, inside, inside],
         scratch_shapes=[
             pltpu.VMEM((2, NX, NZ, CHUNKS, 8, 128), BF16),
@@ -656,16 +705,16 @@
             pltpu.VMEM((4, 128, 256), BF16),
             pltpu.VMEM((4, 64, 2, 256), BF16),
             pltpu.VMEM((27, 64, 256), F32),
-            pltpu.SemaphoreType.DMA((12,)),
+            pltpu.SemaphoreType.DMA((12 + CHUNKS,)),
         ],
-    )(total, frames_grad, latent)
+    )(total, frames_grad, latent, note)
 
 
 def on_device(frames, norm_gain, conv_weight, conv_bias, latent_grad):
-    frames_grad, latent, total = whole(
+    frames_grad, latent, total, note = whole(
         latent_grad, frames, norm_gain.reshape(1, 256), conv_weight.reshape(3, 9, 256, 256), conv_bias.reshape(1, 256),
     )
-    weight_grad, frames_grad, latent, gain_grad, bias_grad = finish(total, frames_grad, latent)
+    weight_grad, frames_grad, latent, gain_grad, bias_grad = finish(total, frames_grad, latent, note)
     return (
         latent, frames_grad, weight_grad.reshape(3, 3, 3, 64, 256), gain_grad.reshape(64), bias_grad.reshape(64),
     )

time: 88.2 us -> 93.3 us (1.058)
  Pallas kernels: 87.5 us -> 92.3 us
    pallas_call x1, Pallas kernels: 83.9 us -> 87.9 us  [whole(): pl.pallas_call(whole_kernel, out_shape=(jax.ShapeDtypeStruct((4, 2, 256,...]
where the time goes in v5:
time: 93.3 us; the launch traced here: 93.1 us
  Pallas kernels  92.3 us (99%)
    pallas_call x1, Pallas kernels, whole(): pl.pallas_call(whole_kernel, out_shape=(jax.ShapeDtypeStruct((4, 2, 256,...  87.9 us
    pallas_call x1, Pallas kernels, finish(): pl.pallas_call(finish_kernel, out_shape=(jax.ShapeDtypeStruct((27, 64, 25...  4.41 us

profile of v5, /device:TPU:1, one launch (start us, length us, event | category | flops | bytes accessed | tf_op | source)
XLA Modules:
  0.0 93.1 jit_solution(428676605273203911)
XLA Ops:
  0.6 87.9 %shard_map.92 = (bf16[4,2,256,256]{3,2,1,0:T(8,128)(2,1)}, bf16[4,128,256]{2,1,0:T(8,128)(2,1)}, bf16[2,4,8,7,8,128]{5,4,3,2,1,0:T(8,128)(2,1)}, f32[2,8,128]{2,1,0:T(8,128)}) custom-call(bf16[4,64,2,256]{3,2,1,0:T(2,128)(2,1)} %latent_grad_far.1, bf16[4,2,256,256]{3,2,1,0:T(8,128)(2,1)} %frames_far.1, f32[1,256]{1,0:T(1,128)} %bitcast.8, ...), custom_call_target="tpu_custom_call" | custom-call | flops 5500000256 | bytes 12000000 | tf_op jit(solution)/shard_map/pallas_call | solution.py:562
  88.5 4.4 %shard_map.93 = (f32[27,64,256]{2,1,0:T(8,128)}, bf16[4,2,256,256]{3,2,1,0:T(8,128)(2,1)}, bf16[4,64,2,256]{3,2,1,0:T(2,128)(2,1)}, f32[1,64]{1,0:T(1,128)}, f32[1,64]{1,0:T(1,128)}) custom-call(bf16[2,4,8,7,8,128]{5,4,3,2,1,0:T(8,128)(2,1)} %get-tuple-element.14.total_far, bf16[4,2,256,256]{3,2,1,0:T(8,128)(2,1)} %get-tuple-element.15.frames_far, ...), custom_call_target="tpu_custom_call" | custom-call | tf_op jit(solution)/shard_map/pallas_call | solution.py:691

commit v6 on v5

--- a/solution.py
+++ b/solution.py
@@ -34,9 +34,15 @@
     other, mine, first_plus, first_minus, second_plus, second_minus,
     mid, first_plus2, first_minus2, second_plus2, second_minus2,
     low, arrive, total, block, latent_in, latent_mid, latent_out,
-    weight_sem, gz_sem, gs_sem, near_sem,
-    core_sem, ring_sem, ring2_sem, z_sem, zback_sem, x_sem, pair_sem, lz_sem, ls_sem, note_sem, out_sem,
+    weight_sem, send_sems, near_in, gz_in, gs_in, core_in, ring_in, ring2_in, z_in, zback_in, x_in, pair_in,
+    lz_in, ls_in, note_in, out_sem,
 ):
+    gz_sem, gs_sem, core_sem, ring_sem, ring2_sem, z_sem = (
+        (0, gz_in), (1, gs_in), (2, core_in), (3, ring_in), (4, ring2_in), (5, z_in),
+    )
+    zback_sem, x_sem, pair_sem, lz_sem, ls_sem, note_sem, near_sem = (
+        (6, zback_in), (7, x_in), (8, pair_in), (9, lz_in), (10, ls_in), (11, note_in), (16, near_in),
+    )
     rows_at = lax.axis_index("rows")
     y = lax.axis_index("tm")
     core, x, z = rows_at % 2, (rows_at // 2) % NX, rows_at // (2 * NX)
@@ -97,10 +103,18 @@
     pl.semaphore_wait(barrier, len(friends))
 
     def copy_to(source, target, sems, at, device):
+        family, arrivals = sems
+        if family == 11 or family == 16:
+            family += at[0]
         return pltpu.make_async_remote_copy(
-            src_ref=source, dst_ref=target, send_sem=sems.at[(0, *at)], recv_sem=sems.at[(1, *at)],
+            src_ref=source, dst_ref=target, send_sem=send_sems.at[family], recv_sem=arrivals.at[at],
             device_id=device, device_id_type=MESH,
         )
+
+    def taken(sem, ref):
+        pltpu.make_async_remote_copy(
+            src_ref=ref, dst_ref=ref, send_sem=sem, recv_sem=sem, device_id=sibling, device_id_type=MESH
+        ).wait_recv()
 
     def send(*args):
         copy = copy_to(*args)
@@ -133,7 +147,7 @@
     def hop_two(between, target, sems, step):
         at = (z - step + NZ) % NZ
         return [
-            send(between.at[at, (slab + move) % (2 * NX)], target.at[at, slab], sems, (step, move), along("slab", move))
+            send(between.at[at, (slab + move) % (2 * NX)], target.at[at, slab], sems, (0,), along("slab", move))
             for move in range(1, 2 * NX)
         ]
 
@@ -195,8 +209,7 @@
     spread[...] = jnp.zeros_like(spread)
     gain_sum[...] = jnp.zeros_like(gain_sum)
     weight_in.wait()
-    for copy in g_inner:
-        copy.wait_recv()
+    taken(gs_in.at[0], landed.at[pl.ds(0, 7)])
 
     def put_grad(frame, half, value):
         grad[pl.ds(frame * 128, 128), pl.ds(half * 128, 128)] = value
@@ -285,7 +298,7 @@
 
     def to_owners(chunk):
         shares[chunk] = [
-            send(low.at[chunk, (z + step) % NZ], arrive.at[step, chunk], z_sem, (chunk, step), along("z", step))
+            send(low.at[chunk, (z + step) % NZ], arrive.at[step, chunk], z_sem, (chunk,), along("z", step))
             for step in order[1:]
         ]
 
@@ -379,12 +392,11 @@
     def spread_out(source, bank, me, axis, total_at, stage):
         bank[me] = source
         return [
-            send(bank.at[me], bank.at[me], note_sem, (stage, step), along(axis, step)) for step in range(1, total_at)
+            send(bank.at[me], bank.at[me], note_sem, (stage,), along(axis, step)) for step in range(1, total_at)
         ]
 
-    def collect(copies, bank, total_at):
-        for copy in copies:
-            copy.wait_recv()
+    def collect(stage, bank, total_at):
+        taken(note_in.at[stage], bank.at[pl.ds(0, total_at - 1)])
         value = bank[0]
         for at in range(1, total_at):
             value = value + bank[at]
@@ -407,20 +419,14 @@
     small = jnp.where(spot == 0, gain_local, jnp.where(spot == 1, bias_local, 0.0))
     note[0] = small[:, :128]
     note[1] = small[:, 128:]
-    notes = [send(note.at[1 - core], note_pair, note_sem, (0, 1), sibling)]
+    notes = [send(note.at[1 - core], note_pair, note_sem, (0,), sibling)]
     next_one(6)
-    close_one(5, 0, 3, 1)
-    notes[0].wait_recv()
-    notes_y = spread_out(note[core] + note_pair[...], note_y, y, "y", NY, 1)
     only(has_below, below_own.wait_recv, below_early.wait_recv)
 
     @pl.loop(0, 6)
     def _(at):
         hidden_tile(below.at[at], at, 2, False)
 
-    close_one(2, 4, 6)
-    next_two(5, 0, 3, 1)
-    notes_x = spread_out(collect(notes_y, note_y, NY), note_x, x, "x", NX, 2)
     spread[0] = jnp.broadcast_to(bias[...], (512, 256))
 
     @pl.loop(0, 3)
@@ -428,26 +434,31 @@
         where = pl.ds(pl.multiple_of(tap * 128, 128), 512)
         spread[0] += dot_nn(columns[where, :], weight[tap].reshape(2304, 256))
 
-    next_two(2, 4, 6)
-    close_two(5, 0, 3, 1)
     for frame in range(4):
         for half in range(2):
             woven[frame, half] = spread[0, pl.ds(frame * 128, 128), pl.ds(half * 128, 128)]
     unweave(latent_in)
-    close_two(2, 4, 6)
     outer = hop_one(latent_in, latent_mid, lz_sem)
     latent_mid[z] = latent_in[z]
-    inner = hop_two(latent_mid, latent_out, ls_sem, 0)
-    notes_z = spread_out(collect(notes_x, note_x, NX), note_z, z, "z", NZ, 3)
-    started = list(pair.values()) + g_outer + g_inner + notes + notes_y + notes_x + notes_z
-    for table in (opened, sent, opened2, sent2, shares):
-        for chunk in range(CHUNKS):
-            started += table[chunk]
-
+    hop_two(latent_mid, latent_out, ls_sem, 0)
+    close_one(5, 0, 3, 1)
+    notes[0].wait_recv()
+    spread_out(note[core] + note_pair[...], note_y, y, "y", NY, 1)
+    close_one(2, 4, 6)
+    next_two(5, 0, 3, 1)
+    spread_out(collect(1, note_y, NY), note_x, x, "x", NX, 2)
+    next_two(2, 4, 6)
+    close_two(5, 0, 3, 1)
+    for copy, step in zip(outer, order[1:]):
+        copy.wait_recv()
+        hop_two(latent_mid, latent_out, ls_sem, step)
+    latent_out[:, slab] = latent_mid[:, slab]
+    close_two(2, 4, 6)
+    spread_out(collect(2, note_x, NX), note_z, z, "z", NZ, 3)
     for chunk in (5, 0, 3, 1, 2, 4, 6):
         summed = low[chunk, z]
-        for copy, step in zip(shares[chunk], order[1:]):
-            copy.wait_recv()
+        taken(z_in.at[chunk], low.at[0, pl.ds(0, 7)])
+        for step in order[1:]:
             summed += arrive[step, chunk]
         total[z, chunk] = summed.astype(BF16)
 
@@ -477,7 +488,7 @@
     def across_core(which, step, at):
         source = total.at[at] if which == 0 else block.at[(left, right, across)[which - 1], at]
         where = (x, left, right, across)[which]
-        return copy_to(source, sib.at[where, at], pair_sem, (which, step), sibling)
+        return copy_to(source, sib.at[where, at], pair_sem, (which,), sibling)
 
     def each(body):
         for step in order:
@@ -510,16 +521,11 @@
 
     each(fan_one)
     kept = [frames_out, keep(total, core, x, 1)]
-    for copy, step in zip(outer, order[1:]):
-        copy.wait_recv()
-        inner += hop_two(latent_mid, latent_out, ls_sem, step)
-    latent_out[:, slab] = latent_mid[:, slab]
-    note_end[0] = collect(notes_z, note_z, NZ)
-    note_last = send(note_end.at[0], note_end.at[1], note_sem, (0, 2), sibling)
+    note_end[0] = collect(3, note_z, NZ)
+    note_last = send(note_end.at[0], note_end.at[1], note_sem, (4,), sibling)
     each(fan_two)
     kept += [keep(block.at[left], core, left, 2), keep(block.at[right], core, right, 3)]
-    for copy in inner:
-        copy.wait_recv()
+    taken(ls_in.at[0], latent_out.at[pl.ds(0, 7)])
 
     def put_latent(frame, half, value):
         latent[frame, :, pl.ds(half * 128, 128)] = value
@@ -529,29 +535,24 @@
     kept[-1].start()
     each(fan_three)
     kept.append(keep(block.at[across], core, across, 5))
-    note_last.wait()
+    note_last.wait_recv()
     note_out[core] = note_end[0]
     note_out[1 - core] = note_end[1]
     for which, where in enumerate((x, left, right, across)):
-        for step in order:
-            across_core(which, step, (z - step + NZ) % NZ).wait_recv()
+        taken(pair_in.at[which], sib.at[0])
         kept.append(keep(sib.at[where], 1 - core, where, 6 + which))
-    for copy in started + outer + inner:
-        copy.wait_send()
-    for step in order:
-        at = (z - step + NZ) % NZ
-        for which in range(4):
-            across_core(which, step, at).wait_send()
-        to_right(step, at).wait_send()
-        to_left(step, at).wait_send()
-        on_right(step, at).wait_send()
-        on_left(step, at).wait_send()
+    seven, three = pl.ds(0, 7), pl.ds(0, 3)
+    for family, ref in (
+        (0, middle.at[seven]), (1, landed.at[seven]), (2, other), (3, mine.at[:, three]), (4, mid.at[:, three]),
+        (5, low.at[:, seven]), (6, total.at[seven]), (7, block.at[three]), (8, sib),
+        (9, latent_mid.at[seven]), (10, latent_out.at[seven]),
+        (11, note_pair), (12, note_y.at[three]), (13, note_x.at[three]), (14, note_z.at[seven]), (15, note_pair),
+    ):
+        taken(send_sems.at[family], ref)
     only(has_future, early_on.wait_send)
     only(has_above, below_own.wait_send, below_early.wait_send)
     only(has_past, grad_late.wait_send)
     only(has_below, above_own.wait_send, above_late.wait_send)
-    for step in order[1:]:
-        back(step).wait_send()
     for copy in kept:
         copy.wait()
 
@@ -617,19 +618,20 @@
             vmem((NZ, 2 * NX, 8, 256), BF16),
             vmem((NZ, 2 * NX, 8, 256), BF16),
             dma((3,)),
-            dma((2, NZ)),
-            dma((2, NZ, 2 * NX)),
-            dma((2, 6)),
-            dma((2, CHUNKS)),
-            dma((2, CHUNKS, 4)),
-            dma((2, CHUNKS, 4)),
-            dma((2, CHUNKS, NZ)),
-            dma((2, NZ)),
-            dma((2, 4, NZ)),
-            dma((2, 4, NZ)),
-            dma((2, NZ)),
-            dma((2, NZ, 2 * NX)),
-            dma((2, 4, NZ)),
+            dma((22,)),
+            dma((6,)),
+            dma((NZ,)),
+            dma((1,)),
+            dma((CHUNKS,)),
+            dma((CHUNKS, 4)),
+            dma((CHUNKS, 4)),
+            dma((CHUNKS,)),
+            dma((NZ,)),
+            dma((4, NZ)),
+            dma((4,)),
+            dma((NZ,)),
+            dma((1,)),
+            dma((5,)),
             dma((10,)),
         ],
         compiler_params=pltpu.CompilerParams(collective_id=1, has_side_effects=True),
@@ -642,18 +644,15 @@
     total, frames_near, latent_near, latent_wide, wide, sems,
 ):
     copy = pltpu.make_async_copy
-    totals_in = [
-        copy(total_far.at[:, :, :, chunk], total.at[:, :, :, chunk], sems.at[12 + chunk]) for chunk in range(CHUNKS)
-    ]
+    total_in = copy(total_far, total, sems.at[0])
     frames_in = copy(frames_far, frames_near, sems.at[1])
     latent_in = copy(latent_far, latent_near, sems.at[2])
+    total_in.start()
+    frames_in.start()
     latent_in.start()
-    for item in totals_in:
-        item.start()
-    frames_in.start()
+    total_in.wait()
     going = []
     for chunk in range(CHUNKS):
-        totals_in[chunk].wait()
         for tap in range(chunk * TAPS, min(27, chunk * TAPS + TAPS)):
             for core in range(2):
                 for x in range(NX):
@@ -705,7 +704,7 @@
             pltpu.VMEM((4, 128, 256), BF16),
             pltpu.VMEM((4, 64, 2, 256), BF16),
             pltpu.VMEM((27, 64, 256), F32),
-            pltpu.SemaphoreType.DMA((12 + CHUNKS,)),
+            pltpu.SemaphoreType.DMA((12,)),
         ],
     )(total, frames_grad, latent, note)
 

time: 93.3 us -> 84.6 us (0.907)
  Pallas kernels: 92.3 us -> 83.7 us
    pallas_call x1, Pallas kernels: 87.9 us -> 79.5 us  [whole(): pl.pallas_call(whole_kernel, out_shape=(jax.ShapeDtypeStruct((4, 2, 256,...]
where the time goes in v6:
time: 84.6 us; the launch traced here: 84.3 us
  Pallas kernels  83.7 us (99%)
    pallas_call x1, Pallas kernels, whole(): pl.pallas_call(whole_kernel, out_shape=(jax.ShapeDtypeStruct((4, 2, 256,...  79.5 us
    pallas_call x1, Pallas kernels, finish(): pl.pallas_call(finish_kernel, out_shape=(jax.ShapeDtypeStruct((27, 64, 25...  4.18 us

profile of v6, /device:TPU:1, one launch (start us, length us, event | category | flops | bytes accessed | tf_op | source)
XLA Modules:
  0.0 84.3 jit_solution(6095486576592468567)
XLA Ops:
  0.6 79.5 %shard_map.92 = (bf16[4,2,256,256]{3,2,1,0:T(8,128)(2,1)}, bf16[4,128,256]{2,1,0:T(8,128)(2,1)}, bf16[2,4,8,7,8,128]{5,4,3,2,1,0:T(8,128)(2,1)}, f32[2,8,128]{2,1,0:T(8,128)}) custom-call(bf16[4,64,2,256]{3,2,1,0:T(2,128)(2,1)} %latent_grad_far.1, bf16[4,2,256,256]{3,2,1,0:T(8,128)(2,1)} %frames_far.1, f32[1,256]{1,0:T(1,128)} %bitcast.8, ...), custom_call_target="tpu_custom_call" | custom-call | flops 5500000256 | bytes 12000000 | tf_op jit(solution)/shard_map/pallas_call | solution.py:563
  80.1 4.2 %shard_map.93 = (f32[27,64,256]{2,1,0:T(8,128)}, bf16[4,2,256,256]{3,2,1,0:T(8,128)(2,1)}, bf16[4,64,2,256]{3,2,1,0:T(2,128)(2,1)}, f32[1,64]{1,0:T(1,128)}, f32[1,64]{1,0:T(1,128)}) custom-call(bf16[2,4,8,7,8,128]{5,4,3,2,1,0:T(8,128)(2,1)} %get-tuple-element.14.total_far, bf16[4,2,256,256]{3,2,1,0:T(8,128)(2,1)} %get-tuple-element.15.frames_far, ...), custom_call_target="tpu_custom_call" | custom-call | tf_op jit(solution)/shard_map/pallas_call | solution.py:690

commit v7 on v6

--- a/solution.py
+++ b/solution.py
@@ -154,7 +154,6 @@
     g_outer = hop_one(blocks, middle, gz_sem)
     frames_in.wait()
     only(has_future, early_on.start)
-    only(has_above, below_own.start)
     middle[z] = blocks[z]
     g_inner = hop_two(middle, landed, gs_sem, 0)
 
@@ -217,6 +216,7 @@
     weave(landed, put_grad)
     only(has_past, grad_late.start)
     only(has_below, above_own.start)
+    only(has_above, below_own.start)
 
     def step_on(which, source, frames_at):
         for at in frames_at:
@@ -350,7 +350,7 @@
     step_on(1, grad_above, range(6))
     before = 0
     parts[:, 27] = jnp.zeros((2, 256, 128), BF16)
-    for chunk in (3, 1, 2, 4, 6):
+    for chunk in (2, 3, 4, 1, 6):
         weight_taps(chunk)
         pair_send(chunk)
         pair_close(before)
@@ -407,9 +407,9 @@
     back_taps(1)
     next_one(5, 0)
     back_taps(2)
-    next_one(3, 1)
+    next_one(2, 3)
     frame_back(0, 2)
-    next_one(2, 4)
+    next_one(4, 1)
     frame_back(2, 4)
     frames_out = pltpu.make_async_copy(frames_grad, frames_grad_far, out_sem.at[0])
     frames_out.start()
@@ -441,21 +441,17 @@
     outer = hop_one(latent_in, latent_mid, lz_sem)
     latent_mid[z] = latent_in[z]
     hop_two(latent_mid, latent_out, ls_sem, 0)
-    close_one(5, 0, 3, 1)
+    close_one(5, 0, 2, 3)
     notes[0].wait_recv()
     spread_out(note[core] + note_pair[...], note_y, y, "y", NY, 1)
-    close_one(2, 4, 6)
-    next_two(5, 0, 3, 1)
+    close_one(4, 1, 6)
+    next_two(5, 0, 2, 3)
     spread_out(collect(1, note_y, NY), note_x, x, "x", NX, 2)
-    next_two(2, 4, 6)
-    close_two(5, 0, 3, 1)
-    for copy, step in zip(outer, order[1:]):
-        copy.wait_recv()
-        hop_two(latent_mid, latent_out, ls_sem, step)
-    latent_out[:, slab] = latent_mid[:, slab]
-    close_two(2, 4, 6)
+    next_two(4, 1, 6)
+    close_two(5, 0, 2, 3)
+    close_two(4, 1, 6)
     spread_out(collect(2, note_x, NX), note_z, z, "z", NZ, 3)
-    for chunk in (5, 0, 3, 1, 2, 4, 6):
+    for chunk in (5, 0, 2, 3, 4, 1, 6):
         summed = low[chunk, z]
         taken(z_in.at[chunk], low.at[0, pl.ds(0, 7)])
         for step in order[1:]:
@@ -467,6 +463,10 @@
 
     for step in order[1:]:
         back(step).start()
+    for copy, step in zip(outer, order[1:]):
+        copy.wait_recv()
+        hop_two(latent_mid, latent_out, ls_sem, step)
+    latent_out[:, slab] = latent_mid[:, slab]
 
     right, left, across = (x + 1) % NX, (x + 3) % NX, (x + 2) % NX
     HALF, REST = pl.ds(0, 4), pl.ds(4, 3)
@@ -662,11 +662,11 @@
         taps = pl.ds(chunk * TAPS, min(27, chunk * TAPS + TAPS) - chunk * TAPS)
         going.append(copy(wide.at[taps], weight_grad.at[taps], sems.at[3 + chunk]))
         going[-1].start()
-        if chunk == 2:
+        if chunk == 0:
             frames_in.wait()
             going.append(copy(frames_near, frames_grad, sems.at[10]))
             going[-1].start()
-        if chunk == 3:
+        if chunk == 1:
             latent_in.wait()
             for frame in range(4):
                 latent_wide[frame] = latent_near[frame].reshape(64, 2, 256)

time: 84.6 us -> 80.6 us (0.953)
  Pallas kernels: 83.7 us -> 79.8 us
    pallas_call x1, Pallas kernels: 79.5 us -> 75.5 us  [whole(): pl.pallas_call(whole_kernel, out_shape=(jax.ShapeDtypeStruct((4, 2, 256,...]
where the time goes in v7:
time: 80.6 us; the launch traced here: 80.5 us
  Pallas kernels  79.8 us (99%)
    pallas_call x1, Pallas kernels, whole(): pl.pallas_call(whole_kernel, out_shape=(jax.ShapeDtypeStruct((4, 2, 256,...  75.5 us
    pallas_call x1, Pallas kernels, finish(): pl.pallas_call(finish_kernel, out_shape=(jax.ShapeDtypeStruct((27, 64, 25...  4.36 us

profile of v7, /device:TPU:1, one launch (start us, length us, event | category | flops | bytes accessed | tf_op | source)
XLA Modules:
  0.0 80.5 jit_solution(16949295736176021751)
XLA Ops:
  0.6 75.5 %shard_map.92 = (bf16[4,2,256,256]{3,2,1,0:T(8,128)(2,1)}, bf16[4,128,256]{2,1,0:T(8,128)(2,1)}, bf16[2,4,8,7,8,128]{5,4,3,2,1,0:T(8,128)(2,1)}, f32[2,8,128]{2,1,0:T(8,128)}) custom-call(bf16[4,64,2,256]{3,2,1,0:T(2,128)(2,1)} %latent_grad_far.1, bf16[4,2,256,256]{3,2,1,0:T(8,128)(2,1)} %frames_far.1, f32[1,256]{1,0:T(1,128)} %bitcast.8, ...), custom_call_target="tpu_custom_call" | custom-call | flops 5500000256 | bytes 12000000 | tf_op jit(solution)/shard_map/pallas_call | solution.py:563
  76.1 4.4 %shard_map.93 = (f32[27,64,256]{2,1,0:T(8,128)}, bf16[4,2,256,256]{3,2,1,0:T(8,128)(2,1)}, bf16[4,64,2,256]{3,2,1,0:T(2,128)(2,1)}, f32[1,64]{1,0:T(1,128)}, f32[1,64]{1,0:T(1,128)}) custom-call(bf16[2,4,8,7,8,128]{5,4,3,2,1,0:T(8,128)(2,1)} %get-tuple-element.14.total_far, bf16[4,2,256,256]{3,2,1,0:T(8,128)(2,1)} %get-tuple-element.15.frames_far, ...), custom_call_target="tpu_custom_call" | custom-call | tf_op jit(solution)/shard_map/pallas_call | solution.py:690

commit v8 on v7

--- a/solution.py
+++ b/solution.py
@@ -26,9 +26,9 @@
 
 
 def whole_kernel(
-    latent_grad_far, frames_far, gain, weight_far, bias,
+    latent_grad_far, frames_far, gain_far, weight_far, bias_far,
     frames_grad_far, latent_far, result, note_out,
-    latent_grad, frames, frames_grad, latent, sib, note, note_pair, note_y, note_x, note_z, note_end,
+    gain, bias, latent_grad, frames, frames_grad, latent, sib, note, note_pair, note_y, note_x, note_z, note_end,
     weight, blocks, middle, landed, flat, woven, grad, grad_above, early, below,
     columns, turned, grad_next, spread, tile, gain_sum, parts,
     other, mine, first_plus, first_minus, second_plus, second_minus,
@@ -73,8 +73,12 @@
     latent_grad_in = pltpu.make_async_copy(latent_grad_far, latent_grad, weight_sem.at[1])
     frames_in = pltpu.make_async_copy(frames_far, frames, weight_sem.at[2])
     weight_in = pltpu.make_async_copy(weight_far, weight, weight_sem.at[0])
+    gain_in = pltpu.make_async_copy(gain_far, gain, weight_sem.at[3])
+    bias_in = pltpu.make_async_copy(bias_far, bias, weight_sem.at[4])
     latent_grad_in.start()
     frames_in.start()
+    gain_in.start()
+    bias_in.start()
     weight_in.start()
     latent_grad_in.wait()
 
@@ -153,6 +157,8 @@
 
     g_outer = hop_one(blocks, middle, gz_sem)
     frames_in.wait()
+    gain_in.wait()
+    bias_in.wait()
     only(has_future, early_on.start)
     middle[z] = blocks[z]
     g_inner = hop_two(middle, landed, gs_sem, 0)
@@ -427,6 +433,9 @@
     def _(at):
         hidden_tile(below.at[at], at, 2, False)
 
+    close_one(5, 0, 2, 3)
+    notes[0].wait_recv()
+    spread_out(note[core] + note_pair[...], note_y, y, "y", NY, 1)
     spread[0] = jnp.broadcast_to(bias[...], (512, 256))
 
     @pl.loop(0, 3)
@@ -441,9 +450,6 @@
     outer = hop_one(latent_in, latent_mid, lz_sem)
     latent_mid[z] = latent_in[z]
     hop_two(latent_mid, latent_out, ls_sem, 0)
-    close_one(5, 0, 2, 3)
-    notes[0].wait_recv()
-    spread_out(note[core] + note_pair[...], note_y, y, "y", NY, 1)
     close_one(4, 1, 6)
     next_two(5, 0, 2, 3)
     spread_out(collect(1, note_y, NY), note_x, x, "x", NX, 2)
@@ -536,8 +542,10 @@
     each(fan_three)
     kept.append(keep(block.at[across], core, across, 5))
     note_last.wait_recv()
-    note_out[core] = note_end[0]
-    note_out[1 - core] = note_end[1]
+    for at in range(2):
+        half = core if at == 0 else 1 - core
+        kept.append(pltpu.make_async_copy(note_end.at[at], note_out.at[half], out_sem.at[10 + at]))
+        kept[-1].start()
     for which, where in enumerate((x, left, right, across)):
         taken(pair_in.at[which], sib.at[0])
         kept.append(keep(sib.at[where], 1 - core, where, 6 + which))
@@ -559,7 +567,7 @@
 
 def whole(latent_grad, frames, gain, weight, bias):
     dma, vmem = pltpu.SemaphoreType.DMA, pltpu.VMEM
-    inside, far = pl.BlockSpec(memory_space=pltpu.VMEM), pl.BlockSpec(memory_space=pl.ANY)
+    far = pl.BlockSpec(memory_space=pl.ANY)
     return pl.pallas_call(
         whole_kernel,
         out_shape=(
@@ -568,9 +576,11 @@
             jax.ShapeDtypeStruct((2, NX, NZ, CHUNKS, 8, 128), BF16),
             jax.ShapeDtypeStruct((2, 8, 128), F32),
         ),
-        in_specs=[far, far, inside, far, inside],
-        out_specs=[far, far, far, inside],
+        in_specs=[far] * 5,
+        out_specs=[far] * 4,
         scratch_shapes=[
+            vmem((1, 256), F32),
+            vmem((1, 256), F32),
             vmem((4, 64, 2, 256), BF16),
             vmem((4, 2, 256, 256), BF16),
             vmem((4, 2, 256, 256), BF16),
@@ -617,7 +627,7 @@
             vmem((NZ, 2 * NX, 8, 256), BF16),
             vmem((NZ, 2 * NX, 8, 256), BF16),
             vmem((NZ, 2 * NX, 8, 256), BF16),
-            dma((3,)),
+            dma((5,)),
             dma((22,)),
             dma((6,)),
             dma((NZ,)),
@@ -632,7 +642,7 @@
             dma((NZ,)),
             dma((1,)),
             dma((5,)),
-            dma((10,)),
+            dma((12,)),
         ],
         compiler_params=pltpu.CompilerParams(collective_id=1, has_side_effects=True),
         cost_estimate=pl.CostEstimate(flops=5_500_000_000, bytes_accessed=12_000_000, transcendentals=2_000_000),
@@ -640,18 +650,32 @@
 
 
 def finish_kernel(
-    total_far, frames_far, latent_far, note, weight_grad, frames_grad, latent, gain_grad, bias_grad,
-    total, frames_near, latent_near, latent_wide, wide, sems,
+    total_far, frames_far, latent_far, note_far, weight_grad, frames_grad, latent, gain_far, bias_far,
+    note, gain_grad, bias_grad, total, frames_near, latent_near, latent_wide, wide, sems,
 ):
     copy = pltpu.make_async_copy
     total_in = copy(total_far, total, sems.at[0])
     frames_in = copy(frames_far, frames_near, sems.at[1])
     latent_in = copy(latent_far, latent_near, sems.at[2])
+    note_in = copy(note_far, note, sems.at[12])
+    note_in.start()
     total_in.start()
     frames_in.start()
     latent_in.start()
+    note_in.wait()
+    for core in range(2):
+        row = note[core]
+        for side in range(2):
+
+            @pl.when(lax.axis_index("tm") == 2 * core + side)
+            def _():
+                gain_grad[...] = row[0:1, 64 * side : 64 * side + 64]
+                bias_grad[...] = row[1:2, 64 * side : 64 * side + 64]
+
+    going = [copy(gain_grad, gain_far, sems.at[13]), copy(bias_grad, bias_far, sems.at[14])]
+    for item in going:
+        item.start()
     total_in.wait()
-    going = []
     for chunk in range(CHUNKS):
         for tap in range(chunk * TAPS, min(27, chunk * TAPS + TAPS)):
             for core in range(2):
@@ -662,31 +686,22 @@
         taps = pl.ds(chunk * TAPS, min(27, chunk * TAPS + TAPS) - chunk * TAPS)
         going.append(copy(wide.at[taps], weight_grad.at[taps], sems.at[3 + chunk]))
         going[-1].start()
-        if chunk == 0:
+        if chunk == 1:
             frames_in.wait()
             going.append(copy(frames_near, frames_grad, sems.at[10]))
             going[-1].start()
-        if chunk == 1:
+        if chunk == 3:
             latent_in.wait()
             for frame in range(4):
                 latent_wide[frame] = latent_near[frame].reshape(64, 2, 256)
             going.append(copy(latent_wide, latent, sems.at[11]))
             going[-1].start()
-    for core in range(2):
-        row = note[core]
-        for side in range(2):
-
-            @pl.when(lax.axis_index("tm") == 2 * core + side)
-            def _():
-                gain_grad[...] = row[0:1, 64 * side : 64 * side + 64]
-                bias_grad[...] = row[1:2, 64 * side : 64 * side + 64]
-
     for item in going:
         item.wait()
 
 
 def finish(total, frames_grad, latent, note):
-    inside, far = pl.BlockSpec(memory_space=pltpu.VMEM), pl.BlockSpec(memory_space=pl.ANY)
+    far = pl.BlockSpec(memory_space=pl.ANY)
     return pl.pallas_call(
         finish_kernel,
         out_shape=(
@@ -696,15 +711,18 @@
             jax.ShapeDtypeStruct((1, 64), F32),
             jax.ShapeDtypeStruct((1, 64), F32),
         ),
-        in_specs=[far] * 3 + [inside],
-        out_specs=[far, far, far, inside, inside],
+        in_specs=[far] * 4,
+        out_specs=[far] * 5,
         scratch_shapes=[
+            pltpu.VMEM((2, 8, 128), F32),
+            pltpu.VMEM((1, 64), F32),
+            pltpu.VMEM((1, 64), F32),
             pltpu.VMEM((2, NX, NZ, CHUNKS, 8, 128), BF16),
             pltpu.VMEM((4, 2, 256, 256), BF16),
             pltpu.VMEM((4, 128, 256), BF16),
             pltpu.VMEM((4, 64, 2, 256), BF16),
             pltpu.VMEM((27, 64, 256), F32),
-            pltpu.SemaphoreType.DMA((12,)),
+            pltpu.SemaphoreType.DMA((15,)),
         ],
     )(total, frames_grad, latent, note)
 

time: 80.6 us -> 79.1 us (0.981)
  Pallas kernels: 79.8 us -> 78.3 us
    pallas_call x1, Pallas kernels: 4.36 us -> 3.1 us  [finish(): pl.pallas_call(finish_kernel, out_shape=(jax.ShapeDtypeStruct((27, 64, 25...]
where the time goes in v8:
time: 79.1 us; the launch traced here: 78.9 us
  Pallas kernels  78.3 us (99%)
    pallas_call x1, Pallas kernels, whole(): pl.pallas_call(whole_kernel, out_shape=(jax.ShapeDtypeStruct((4, 2, 256,...  75.2 us
    pallas_call x1, Pallas kernels, finish(): pl.pallas_call(finish_kernel, out_shape=(jax.ShapeDtypeStruct((27, 64, 25...  3.1 us

profile of v8, /device:TPU:1, one launch (start us, length us, event | category | flops | bytes accessed | tf_op | source)
XLA Modules:
  0.0 78.9 jit_solution(18238058842845878909)
XLA Ops:
  0.6 75.2 %shard_map.92 = (bf16[4,2,256,256]{3,2,1,0:T(8,128)(2,1)}, bf16[4,128,256]{2,1,0:T(8,128)(2,1)}, bf16[2,4,8,7,8,128]{5,4,3,2,1,0:T(8,128)(2,1)}, f32[2,8,128]{2,1,0:T(8,128)}) custom-call(bf16[4,64,2,256]{3,2,1,0:T(2,128)(2,1)} %latent_grad_far.1, bf16[4,2,256,256]{3,2,1,0:T(8,128)(2,1)} %frames_far.1, f32[1,256]{1,0:T(1,128)} %bitcast.8, ...), custom_call_target="tpu_custom_call" | custom-call | flops 5500000256 | bytes 12000000 | tf_op jit(solution)/shard_map/pallas_call | solution.py:571
  75.8 3.1 %shard_map.93 = (f32[27,64,256]{2,1,0:T(8,128)}, bf16[4,2,256,256]{3,2,1,0:T(8,128)(2,1)}, bf16[4,64,2,256]{3,2,1,0:T(2,128)(2,1)}, f32[1,64]{1,0:T(1,128)}, f32[1,64]{1,0:T(1,128)}) custom-call(bf16[2,4,8,7,8,128]{5,4,3,2,1,0:T(8,128)(2,1)} %get-tuple-element.14.total_far, bf16[4,2,256,256]{3,2,1,0:T(8,128)(2,1)} %get-tuple-element.15.frames_far, ...), custom_call_target="tpu_custom_call" | custom-call | tf_op jit(solution)/shard_map/pallas_call | solution.py:705
